TPU v7x, 512 devices: a whole 4x8x8 slice. The times are simulated.
512 devices in a mesh: pair: 32 (over x, z_lo, core), col: 16 (over z_hi, y).
Axes of the slice: x: 4, y: 8, z: 8 (z_hi: 2, z_lo: 4; z = z_hi * 4 + z_lo), core: 2. Of those that a mesh axis runs over, the one named last changes fastest.
Arguments:
- two_rdm: bfloat16 [128, 128, 128, 128], P('pair', None, 'col'), may hold values from -6 to 6
- one_rdm: float32 [128, 128], replicated, may hold values from -6 to 6
- panel_block: int32 [1], replicated, may hold values from 0 to 15
Outputs:
- updated: bfloat16 [128, 128, 128, 128], P('pair', None, 'col')
- triangle: float32 [512, 512], replicated
Inputs may be any that keep to these rules, and one draw needn't show every extreme that they name: The panel's first value of r is 4 * panel_block[0], below 64.
All inputs are finite; a program needn't handle non-finite values.
Results may differ from a plain program's by a relative error of at most 0.007.
Values may be sent and summed in bfloat16 or wider, within the bound.
A program may use at most 64 MiB of HBM per device.

v0:
```python
import jax
import jax.numpy as jnp
from jax import lax
from jax.sharding import PartitionSpec as P

RPAN = 4


def spread(value, axis, root):
    mine = lax.axis_index(axis) == root
    return lax.psum(jnp.where(mine, value, jnp.zeros_like(value)), axis)


def lower_solve(lower_factor, right_side):
    return lax.linalg.triangular_solve(lower_factor, right_side, left_side=True, lower=True)


def build_block(moved, s_index, one_cols):
    orbitals = moved.shape[0]
    diagonal_mask = (s_index[:, None] == jnp.arange(orbitals, dtype=jnp.int32)[None, :]).astype(
        jnp.float32
    )
    combined = diagonal_mask[:, None, None, :] * one_cols[None, :, :, None] - jnp.transpose(
        moved, (3, 1, 2, 0)
    ).astype(jnp.float32)
    return combined.astype(jnp.bfloat16)


def per_device(two_rdm, one_rdm, panel_block):
    q_count, orbitals, r_count, _ = two_rdm.shape
    groups = lax.axis_size("pair")
    s_count = orbitals // groups
    panel_width = RPAN * orbitals
    pair_index = lax.axis_index("pair")
    col_index = lax.axis_index("col")
    first_orb = panel_block[0] * RPAN
    s_index = pair_index * s_count + jnp.arange(s_count, dtype=jnp.int32)
    one_cols = lax.dynamic_slice_in_dim(one_rdm, col_index * r_count, r_count, 1)
    moved = lax.all_to_all(two_rdm, "pair", split_axis=3, concat_axis=0, tiled=True)
    row_count = s_count * orbitals
    col_count = r_count * orbitals
    local_tile = build_block(moved, s_index, one_cols).reshape(row_count, col_count)
    owner_col = first_orb // r_count
    within = first_orb % r_count
    panel_cols = lax.dynamic_slice_in_dim(local_tile, within * orbitals, panel_width, 1)
    panel = spread(panel_cols, "col", owner_col)
    gram_part = lax.dot_general(
        panel, panel, (((0,), (0,)), ((), ())), preferred_element_type=jnp.float32
    )
    gram, sums_t = lax.psum(
        (
            gram_part,
            lax.dot_general(
                local_tile, panel, (((0,), (0,)), ((), ())), preferred_element_type=jnp.float32
            ),
        ),
        "pair",
    )
    lower_factor = jnp.linalg.cholesky(gram)
    weights_t = lower_solve(lower_factor, sums_t.T).T.astype(jnp.bfloat16)
    basis = lower_solve(lower_factor, panel.T.astype(jnp.float32)).T.astype(jnp.bfloat16)
    col_orb = col_index * r_count + jnp.arange(col_count, dtype=jnp.int32) // orbitals
    trailing = col_orb >= first_orb + RPAN
    product = lax.dot_general(
        basis, weights_t, (((1,), (1,)), ((), ())), preferred_element_type=jnp.float32
    )
    refreshed = local_tile.astype(jnp.float32) - product
    result = jnp.where(trailing[None, :], refreshed, local_tile.astype(jnp.float32)).astype(
        jnp.bfloat16
    )
    return (result.reshape(s_count, orbitals, r_count, orbitals), lower_factor.T / orbitals)


def solution(mesh):
    return jax.shard_map(
        per_device,
        mesh=mesh,
        in_specs=(P("pair", None, "col", None), P(), P()),
        out_specs=(P("pair", None, "col", None), P()),
        check_vma=False,
    )
```

profile of v0, /device:TPU:1, one launch (start us, length us, event | category | flops | bytes accessed | tf_op | source)
XLA Modules:
  0.0 708.1 jit_solution(15739630665593860776)
XLA Ops:
  7.2 2.9 copy.17
  10.1 11.4 %all-to-all-start = ((bf16[4,128,8,128]{1,2,0,3:T(8,128)(2,1)}), bf16[4,128,8,128]{1,2,0,3:T(8,128)(2,1)S(1)}, u32[]{:S(2)}, u32[]{:S(2)}) async-start(bf16[4,128,8,128]{1,2,0,3:T(8,128)(2,1)} %copy.17), calls=%async_computation | async-start | bytes 2097152 | tf_op jit(solution)/shard_map/all_to_all | solution.py:39
  22.4 26.9 %all-to-all-done = bf16[4,128,8,128]{1,2,0,3:T(8,128)(2,1)S(1)} async-done(((bf16[4,128,8,128]{1,2,0,3:T(8,128)(2,1)}), bf16[4,128,8,128]{1,2,0,3:T(8,128)(2,1)S(1)}, u32[]{:S(2)}, u32[]{:S(2)}) %all-to-all-start) | async-done | bytes 1048608 | tf_op jit(solution)/shard_map/all_to_all | solution.py:39
  49.4 0.2 copy.18
  49.6 0.3 convert_bitcast_fusion
  49.8 0.2 copy.19
  50.1 0.9 fusion.1
  51.0 0.4 copy.20
  51.4 0.2 copy.33
  51.6 0.9 dynamic-slice_select_fusion
  52.5 0.5 all-reduce.7.cloned.1.call-start
  53.0 185.3 %all-reduce.5.cloned.1.call-done = bf16[512,512]{0,1:T(8,128)(2,1)} async-done(((bf16[512,512]{0,1:T(8,128)(2,1)}), bf16[512,512]{0,1:T(8,128)(2,1)}) %all-reduce.5.cloned.1.call-update) | async-done | bytes 524304 | tf_op jit(solution)/shard_map/psum | solution.py:11
  238.3 3.2 fusion.74
  241.4 1.4 fusion.82
  242.9 1.1 bitcast_convert_fusion
  244.1 299.5 %all-reduce.7.cloned.1.call-done = (f32[512,1024]{1,0:T(8,128)}, f32[512,512]{0,1:T(8,128)}) async-done(((f32[512,1024]{1,0:T(8,128)}, f32[512,512]{0,1:T(8,128)}), (f32[512,1024]{1,0:T(8,128)}, f32[512,512]{0,1:T(8,128)})) %all-reduce.7.cloned.1.call-update) | async-done | bytes 3145744 | tf_op jit(solution)/shard_map/psum | solution.py:50
  543.6 2.6 copy.22
  546.2 1.4 fusion.21
  547.6 1.0 copy-done.6
  548.6 11.7 %cholesky.104 = f32[128,128]{1,0:T(8,128)S(1)} custom-call(f32[128,128]{1,0:T(8,128)S(1)} %cholesky.266), custom_call_target="Cholesky" | custom-call | tf_op jit(solution)/shard_map/jit(cholesky)/cholesky | solution.py:59
  560.5 9.8 %custom-call.32 = f32[1,128,128]{1,2,0:T(8,128)S(1)} custom-call(f32[1,128,128]{2,1,0:T(8,128)S(1)} %get-tuple-element.39), custom_call_target="InvertDiagBlocksLowerTriangular" | custom-call | tf_op jit(solution)/shard_map/jit(cholesky)/cholesky | solution.py:59
  570.3 1.2 constant_dynamic-update-slice_fusion.3
  571.6 1.3 convolution_subtract_fusion.5
  572.8 11.7 %cholesky.217 = f32[128,128]{1,0:T(8,128)S(1)} custom-call(f32[128,128]{1,0:T(8,128)S(1)} %cholesky.270), custom_call_target="Cholesky" | custom-call | tf_op jit(solution)/shard_map/jit(cholesky)/cholesky | solution.py:59
  584.6 9.9 %custom-call.33 = f32[1,128,128]{1,2,0:T(8,128)S(1)} custom-call(f32[1,128,128]{2,1,0:T(8,128)S(1)} %get-tuple-element.36), custom_call_target="InvertDiagBlocksLowerTriangular" | custom-call | tf_op jit(solution)/shard_map/jit(cholesky)/cholesky | solution.py:59
  594.5 0.3 convolution_dynamic-update-slice_fusion
  594.8 1.3 convolution_subtract_fusion.6
  596.1 11.7 %cholesky.238 = f32[128,128]{1,0:T(8,128)S(1)} custom-call(f32[128,128]{1,0:T(8,128)S(1)} %cholesky.275), custom_call_target="Cholesky" | custom-call | tf_op jit(solution)/shard_map/jit(cholesky)/cholesky | solution.py:59
  607.8 0.7 compare_reduce_fusion.1
  608.5 9.8 %custom-call.34 = f32[1,128,128]{1,2,0:T(8,128)S(1)} custom-call(f32[1,128,128]{2,1,0:T(8,128)S(1)} %get-tuple-element.33), custom_call_target="InvertDiagBlocksLowerTriangular" | custom-call | tf_op jit(solution)/shard_map/jit(cholesky)/cholesky | solution.py:59
  618.3 0.2 convolution_dynamic-update-slice_fusion.1
  618.5 1.2 convolution_subtract_fusion.7
  619.8 11.9 %cholesky.255 = f32[128,128]{1,0:T(8,128)S(1)} custom-call(f32[128,128]{1,0:T(8,128)S(1)} %convolution_subtract_fusion.7), custom_call_target="Cholesky" | custom-call | tf_op jit(solution)/shard_map/jit(cholesky)/cholesky | solution.py:59
  631.7 0.7 compare_reduce_fusion
  632.4 0.6 compare_reduce_fusion.2
  635.5 1.6 multiply_bitcast_fusion
  637.1 11.4 %while.1 = (s32[]{:T(128)}, f32[512,512]{1,0:T(8,128)}, s32[4,2]{0,1:T(2,128)S(1)}, f32[4,128,128]{2,1,0:T(8,128)S(1)}, s32[]{:T(128)}) while((s32[]{:T(128)}, f32[512,512]{1,0:T(8,128)}, s32[4,2]{0,1:T(2,128)S(1)}, f32[4,128,128]{2,1,0:T(8,128)S(1)}, s32[]{:T(128)}) %tuple.41), condition=%wide.while_cond, body=%wide.while_body.sunk | while | flops 2 | bytes 131181 | solution.py:15
  637.2 0.5 fusion.96
  637.7 2.2 bitcast_dynamic-update-slice_fusion.2
  640.1 0.5 fusion.96
  640.6 2.2 bitcast_dynamic-update-slice_fusion.2
  642.9 0.5 fusion.96
  643.5 2.2 bitcast_dynamic-update-slice_fusion.2
  645.8 0.5 fusion.96
  646.3 2.2 bitcast_dynamic-update-slice_fusion.2
  648.5 39.3 %custom-call.35 = f32[4,128,128]{1,2,0:T(8,128)S(1)} custom-call(f32[4,128,128]{2,1,0:T(8,128)S(1)} %get-tuple-element.9), custom_call_target="InvertDiagBlocksLowerTriangular" | custom-call | tf_op jit(solution)/shard_map/triangular_solve | solution.py:15
  687.9 0.3 fusion.81
  688.2 1.4 convolution_subtract_fusion.3
  689.5 0.4 fusion.80
  690.0 0.4 convolution_subtract_fusion.2
  690.4 0.4 fusion.79
  690.9 0.6 convolution_subtract_fusion.4
  691.5 0.4 convolution_convert_fusion.1
  691.9 0.6 fusion.78
  692.6 0.6 convolution_subtract_fusion.1
  693.2 0.6 fusion.77
  693.8 0.7 convolution_subtract_fusion
  694.5 0.6 fusion.76
  695.2 1.1 fusion.8
  696.3 0.6 convolution_convert_fusion
  696.9 0.8 fusion
  697.7 0.3 reshape.98
  698.0 1.7 copy.24
  699.7 1.3 copy.25
  (38 shorter events, 0.9 us)
Async XLA Ops:
  7.2 15.1 %copy-start = (f32[128,128]{1,0:T(8,128)S(1)}, f32[128,128]{1,0:T(8,128)}, u32[]{:S(2)}) copy-start(f32[128,128]{1,0:T(8,128)} %param.4) | copy-start | bytes 196612
  10.1 39.3 %all-to-all-start = ((bf16[4,128,8,128]{1,2,0,3:T(8,128)(2,1)}), bf16[4,128,8,128]{1,2,0,3:T(8,128)(2,1)S(1)}, u32[]{:S(2)}, u32[]{:S(2)}) async-start(bf16[4,128,8,128]{1,2,0,3:T(8,128)(2,1)} %copy.17), calls=%async_computation | async-start | bytes 2097152 | tf_op jit(solution)/shard_map/all_to_all | solution.py:39
  21.5 216.8 %all-reduce.5.cloned.1.call-start = ((), (), s32[]{:S(2)}) async-start(), calls=%async_computation.1 | async-start | bytes 1048576 | tf_op jit(solution)/shard_map/psum | solution.py:11
  52.5 491.1 %all-reduce.7.cloned.1.call-start = ((), (), s32[]{:S(2)}) async-start(), calls=%async_computation.2 | async-start | bytes 6291456 | tf_op jit(solution)/shard_map/psum | solution.py:50
  238.3 3.2 copy-start.1
  543.6 2.6 copy-start.3
  547.6 1.0 copy-start.6
  648.5 41.5 %copy-start.2 = (f32[512,512]{1,0:T(8,128)S(1)}, f32[512,512]{1,0:T(8,128)}, u32[]{:S(2)}) copy-start(f32[512,512]{1,0:T(8,128)} %get-tuple-element.108) | copy-start | bytes 3145732
  687.8 2.2 copy-start.5
  690.0 2.0 copy-start.7
  697.7 2.0 copy-start.4
Sparse Core Ops, SparseCore 0:
  52.6 185.6 all-reduce.4
  243.0 300.4 all-reduce.6
where the time goes:
time: 712 us; the launch traced here: 708 us
  waiting for transfers between devices  512 us (72%)
  other arithmetic  124 us (17%)
  local copies, waits for them, and re-layouts  22.5 us (3%)
  matrix products  19.8 us (3%)
  between operations  17.9 us (3%)
  starting transfers between devices  11.9 us (2%)
    psum x1, waiting for transfers between devices, per_device(): lax.psum((gram_part, lax.dot_general(local_tile, panel, (((0,), (0,)), ((...  300 us
    psum x1, waiting for transfers between devices, spread(): return lax.psum(jnp.where(mine, value, jnp.zeros_like(value)), axis)  185 us
    another operation x14, other arithmetic, per_device(): lower_factor = jnp.linalg.cholesky(gram)  78.7 us
    another operation x2, other arithmetic, lower_solve(): lax.linalg.triangular_solve(lower_factor, right_side, left_side=True, low...  39.3 us
    all_to_all x1, waiting for transfers between devices, per_device(): lax.all_to_all(two_rdm, 'pair', split_axis=3, concat_axis=0, tiled=True)  26.9 us
  transfers between devices with their start and end apart: 3, of which 3 were waited for; matrix products, arithmetic and copies ran while one was open for 0% of the time, Pallas kernels for 0%

commit v1 on v0

v1 whole, which is shorter than its diff:
```python
import functools

import jax
import jax.numpy as jnp
from jax import lax
from jax.experimental import pallas as pl
from jax.experimental.pallas import tpu as pltpu
from jax.sharding import PartitionSpec as P

RPAN = 4
BLOCK = 128
STRIP = 4
EXACT = lax.Precision.HIGHEST


def factor_block(work):
    for k in range(0, BLOCK, STRIP):
        r0 = (k // 8) * 8
        left = work[r0:BLOCK, 0:BLOCK]
        cols = [jnp.broadcast_to(left[:, k + j : k + j + 1], (BLOCK - r0, BLOCK)) for j in range(STRIP)]
        rows = [work[k + j : k + j + 1, :] for j in range(STRIP)]
        entry = {(i, j): cols[j][k + i - r0 : k + i - r0 + 1, :] for j in range(STRIP) for i in range(j, STRIP)}
        for j in range(STRIP):
            inv = lax.rsqrt(entry[j, j])
            rows[j] = rows[j] * jnp.concatenate([inv, inv], axis=1)
            cols[j] = cols[j] * inv
            low = {i: entry[i, j] * inv for i in range(j + 1, STRIP)}
            for i in range(j + 1, STRIP):
                for m in range(j + 1, i + 1):
                    entry[i, m] = entry[i, m] - low[i] * low[m]
                rows[i] = rows[i] - jnp.concatenate([low[i], low[i]], axis=1) * rows[j]
                cols[i] = cols[i] - low[i] * cols[j]
        for j in range(STRIP):
            work[k + j : k + j + 1, :] = rows[j]
        t0 = k + STRIP
        if t0 < BLOCK:
            s0 = (t0 // 8) * 8
            delta_a, delta_b = 0.0, 0.0
            for j in range(STRIP):
                c = cols[j][s0 - r0 :, :]
                delta_a = delta_a + c * rows[j][:, :BLOCK]
                delta_b = delta_b + c * rows[j][:, BLOCK:]
            if s0 < t0:
                below = lax.broadcasted_iota(jnp.int32, (BLOCK - s0, BLOCK), 0) + s0 >= t0
                delta_a = jnp.where(below, delta_a, 0.0)
                delta_b = jnp.where(below, delta_b, 0.0)
            work[s0:BLOCK, :BLOCK] = work[s0:BLOCK, :BLOCK] - delta_a
            work[s0:BLOCK, BLOCK:] = work[s0:BLOCK, BLOCK:] - delta_b


def factor_kernel(scale, gram_ref, tri_ref, inv_ref, aug, work):
    n = gram_ref.shape[0]
    row = lax.broadcasted_iota(jnp.int32, (n, n), 0)
    col = lax.broadcasted_iota(jnp.int32, (n, n), 1)
    aug[:, :n] = gram_ref[...]
    aug[:, n:] = (row == col).astype(jnp.float32)
    eye = (
        lax.broadcasted_iota(jnp.int32, (BLOCK, BLOCK), 0) == lax.broadcasted_iota(jnp.int32, (BLOCK, BLOCK), 1)
    ).astype(jnp.float32)

    def step(b, carry):
        o = pl.multiple_of(b * BLOCK, BLOCK)
        work[:, :BLOCK] = aug[pl.ds(o, BLOCK), pl.ds(o, BLOCK)]
        work[:, BLOCK:] = eye
        factor_block(work)
        aug[pl.ds(o, BLOCK), :] = jnp.dot(
            work[:, BLOCK:], aug[pl.ds(o, BLOCK), :], precision=EXACT, preferred_element_type=jnp.float32
        )

        def trail(m, carry):
            q = pl.multiple_of(m * BLOCK, BLOCK)
            u = aug[pl.ds(o, BLOCK), pl.ds(q, BLOCK)]
            aug[pl.ds(q, BLOCK), :] -= lax.dot_general(
                u, aug[pl.ds(o, BLOCK), :], (((0,), (0,)), ((), ())), precision=EXACT, preferred_element_type=jnp.float32
            )
            return carry

        return lax.fori_loop(b + 1, n // BLOCK, trail, carry)

    lax.fori_loop(0, n // BLOCK, step, 0)
    tri_ref[...] = jnp.where(row <= col, aug[:, :n], 0.0) / scale
    inv_ref[...] = jnp.where(row >= col, aug[:, n:], 0.0)


def factor(gram, scale):
    n = gram.shape[0]
    whole = pl.BlockSpec(memory_space=pltpu.VMEM)
    return pl.pallas_call(
        functools.partial(factor_kernel, scale),
        out_shape=(jax.ShapeDtypeStruct((n, n), jnp.float32),) * 2,
        in_specs=[whole],
        out_specs=(whole,) * 2,
        scratch_shapes=[pltpu.VMEM((n, 2 * n), jnp.float32), pltpu.VMEM((BLOCK, 2 * BLOCK), jnp.float32)],
        compiler_params=pltpu.CompilerParams(vmem_limit_bytes=16 << 20),
        cost_estimate=pl.CostEstimate(flops=4 * n**3, bytes_accessed=12 * n * n, transcendentals=n),
        name="panel_factor",
    )(gram)


def share(value, axis):
    count = lax.axis_size(axis)
    return lax.all_to_all(jnp.broadcast_to(value[None], (count, *value.shape)), axis, 0, 0)


def collect(value, axis):
    count = lax.axis_size(axis)
    return lax.all_to_all(value.reshape(count, value.shape[0] // count, *value.shape[1:]), axis, 0, 0)


def build_block(moved, s_index, one_cols):
    orbitals = moved.shape[0]
    diagonal_mask = (s_index[:, None] == jnp.arange(orbitals, dtype=jnp.int32)[None, :]).astype(jnp.float32)
    combined = diagonal_mask[:, None, None, :] * one_cols[None, :, :, None] - jnp.transpose(
        moved, (3, 1, 2, 0)
    ).astype(jnp.float32)
    return combined.astype(jnp.bfloat16)


def per_device(two_rdm, one_rdm, panel_block):
    q_count, orbitals, r_count, _ = two_rdm.shape
    groups = lax.axis_size("pair")
    s_count = orbitals // groups
    panel_width = RPAN * orbitals
    pair_index = lax.axis_index("pair")
    col_index = lax.axis_index("col")
    first_orb = panel_block[0] * RPAN
    s_index = pair_index * s_count + jnp.arange(s_count, dtype=jnp.int32)
    one_cols = lax.dynamic_slice_in_dim(one_rdm, col_index * r_count, r_count, 1)
    moved = lax.all_to_all(two_rdm, "pair", split_axis=3, concat_axis=0, tiled=True)
    row_count = s_count * orbitals
    col_count = r_count * orbitals
    local_tile = build_block(moved, s_index, one_cols).reshape(row_count, col_count)
    owner_col = first_orb // r_count
    within = first_orb % r_count
    panel_cols = lax.dynamic_slice_in_dim(local_tile, within * orbitals, panel_width, 1)
    mine = lax.dynamic_index_in_dim(collect(panel_cols, "col"), owner_col, 0, keepdims=False)
    panel = share(mine, "col").reshape(row_count, panel_width)
    gram_part = lax.dot_general(panel, panel, (((0,), (0,)), ((), ())), preferred_element_type=jnp.float32)
    gram = share(collect(gram_part, "pair").sum(0), "pair").reshape(panel_width, panel_width)
    triangle, inverse = factor(gram, orbitals)
    sums_part = lax.dot_general(
        local_tile, panel, (((0,), (0,)), ((), ())), preferred_element_type=jnp.float32
    ).astype(jnp.bfloat16)
    sums_mine = collect(sums_part, "pair").astype(jnp.float32).sum(0).astype(jnp.bfloat16)
    sums_t = share(sums_mine, "pair").reshape(col_count, panel_width)
    inverse_hi = inverse.astype(jnp.bfloat16)
    inverse_lo = (inverse - inverse_hi.astype(jnp.float32)).astype(jnp.bfloat16)

    def solve_right(value):
        dims = (((1,), (1,)), ((), ()))
        return (
            lax.dot_general(value, inverse_hi, dims, preferred_element_type=jnp.float32)
            + lax.dot_general(value, inverse_lo, dims, preferred_element_type=jnp.float32)
        ).astype(jnp.bfloat16)

    weights_t = solve_right(sums_t)
    basis = solve_right(panel)
    col_orb = col_index * r_count + jnp.arange(col_count, dtype=jnp.int32) // orbitals
    trailing = col_orb >= first_orb + RPAN
    product = lax.dot_general(basis, weights_t, (((1,), (1,)), ((), ())), preferred_element_type=jnp.float32)
    refreshed = local_tile.astype(jnp.float32) - product
    result = jnp.where(trailing[None, :], refreshed, local_tile.astype(jnp.float32)).astype(jnp.bfloat16)
    return (result.reshape(s_count, orbitals, r_count, orbitals), triangle)


def solution(mesh):
    return jax.shard_map(
        per_device,
        mesh=mesh,
        in_specs=(P("pair", None, "col", None), P(), P()),
        out_specs=(P("pair", None, "col", None), P()),
        check_vma=False,
    )
```

time: 712 us -> 242 us (0.34)
  waiting for transfers between devices: 512 us -> 128 us
  other arithmetic: 124 us -> 1.42 us
  starting transfers between devices: 11.9 us -> 42.9 us
  Pallas kernels: 0 us -> 24.3 us
  blocking collectives: 0 us -> 23.2 us
  between operations: 17.9 us -> 1.53 us
  local copies, waits for them, and re-layouts: 22.5 us -> 9.56 us
  matrix products: 19.8 us -> 11 us
    psum x2 -> x0, waiting for transfers between devices: 485 us -> none  [the longest x1 300 us: per_device(): lax.psum((gram_part, lax.dot_general(local_tile, panel, (((0,), (0,)), ((...]
    another operation x16 -> x0, other arithmetic: 118 us -> none  [the longest x14 78.7 us: per_device(): lower_factor = jnp.linalg.cholesky(gram)]
    all_to_all x0 -> x5, waiting for transfers between devices: none -> 101 us  [the longest x3 71.7 us: collect(): lax.all_to_all(value.reshape(count, value.shape[0] // count, *value.shape...]
    all_to_all x0 -> x5, starting transfers between devices: none -> 31.6 us  [the longest x3 23.7 us: collect(): lax.all_to_all(value.reshape(count, value.shape[0] // count, *value.shape...]
    pallas_call x0 -> x1, Pallas kernels: none -> 24.3 us  [factor(): pl.pallas_call(functools.partial(factor_kernel, scale), out_shape=(jax.Sh...]
    all_to_all x0 -> x1, blocking collectives: none -> 23.2 us  [share(): lax.all_to_all(jnp.broadcast_to(value[None], (count, *value.shape)), axis...]
    another operation x20 -> x0, matrix products: 14.4 us -> none  [the longest x14 8.93 us: lower_solve(): lax.linalg.triangular_solve(lower_factor, right_side, left_side=True, low...]
    another operation x17 -> x0, local copies, waits for them, and re-layouts: 11.5 us -> none
  transfers between devices with their start and end apart: 3 -> 6, of which waited for: 3 -> 6; matrix products, arithmetic and copies ran while one was open for 0% -> 2% of each run, Pallas kernels for 0% -> 10%
where the time goes in v1:
time: 242 us
  waiting for transfers between devices  128 us (53%)
  starting transfers between devices  42.9 us (18%)
  Pallas kernels  24.3 us (10%)
  blocking collectives  23.2 us (10%)
  matrix products  11 us (5%)
  local copies, waits for them, and re-layouts  9.56 us (4%)
    all_to_all x3, waiting for transfers between devices, collect(): lax.all_to_all(value.reshape(count, value.shape[0] // count, *value.shape...  71.7 us
    all_to_all x2, waiting for transfers between devices, share(): lax.all_to_all(jnp.broadcast_to(value[None], (count, *value.shape)), axis...  28.9 us
    all_to_all x1, waiting for transfers between devices, per_device(): lax.all_to_all(two_rdm, 'pair', split_axis=3, concat_axis=0, tiled=True)  27 us
    pallas_call x1, Pallas kernels, factor(): pl.pallas_call(functools.partial(factor_kernel, scale), out_shape=(jax.Sh...  24.3 us
    all_to_all x3, starting transfers between devices, collect(): lax.all_to_all(value.reshape(count, value.shape[0] // count, *value.shape...  23.7 us
    all_to_all x1, blocking collectives, share(): lax.all_to_all(jnp.broadcast_to(value[None], (count, *value.shape)), axis...  23.2 us
    all_to_all x1, starting transfers between devices, per_device(): lax.all_to_all(two_rdm, 'pair', split_axis=3, concat_axis=0, tiled=True)  11.4 us
    all_to_all x2, starting transfers between devices, share(): lax.all_to_all(jnp.broadcast_to(value[None], (count, *value.shape)), axis...  7.82 us
  transfers between devices with their start and end apart: 6, of which 6 were waited for; matrix products, arithmetic and copies ran while one was open for 2% of the time, Pallas kernels for 10%

profile of v1, /device:TPU:1, one launch (start us, length us, event | category | flops | bytes accessed | tf_op | source)
XLA Modules:
  0.0 241.5 jit_solution(733645274975894743)
XLA Ops:
  0.6 0.0 copy-start
  0.6 2.9 %copy.13 = bf16[4,128,8,128]{1,2,0,3:T(8,128)(2,1)} copy(bf16[4,128,8,128]{3,2,1,0:T(8,128)(2,1)} %param.3) | data formatting | bytes 2097152 | tf_op args[0]
  3.6 11.4 %all-to-all-start = ((bf16[4,128,8,128]{1,2,0,3:T(8,128)(2,1)}), bf16[4,128,8,128]{1,2,0,3:T(8,128)(2,1)S(1)}, u32[]{:S(2)}, u32[]{:S(2)}) async-start(bf16[4,128,8,128]{1,2,0,3:T(8,128)(2,1)} %copy.13), calls=%async_computation | async-start | bytes 2097152 | tf_op jit(solution)/shard_map/all_to_all | solution.py:129
  15.6 0.0 copy-done
  15.7 0.1 constant_dynamic-slice_fusion.1
  15.7 0.1 copy.12
  15.8 27.0 %all-to-all-done = bf16[4,128,8,128]{1,2,0,3:T(8,128)(2,1)S(1)} async-done(((bf16[4,128,8,128]{1,2,0,3:T(8,128)(2,1)}), bf16[4,128,8,128]{1,2,0,3:T(8,128)(2,1)S(1)}, u32[]{:S(2)}, u32[]{:S(2)}) %all-to-all-start) | async-done | bytes 1048608 | tf_op jit(solution)/shard_map/all_to_all | solution.py:129
  42.8 0.2 copy.14
  43.0 0.3 convert_bitcast_fusion
  43.3 0.2 copy.15
  43.6 0.9 fusion.1
  44.4 1.2 copy.16
  45.7 0.0 copy-start.3
  45.7 0.3 copy.24
  46.0 0.9 constant_dynamic-slice_fusion
  46.8 12.7 %all-to-all-start.1 = ((bf16[16,32,512]{2,1,0:T(8,128)(2,1)}), bf16[16,32,512]{2,1,0:T(8,128)(2,1)S(1)}, u32[]{:S(2)}, u32[]{:S(2)}) async-start(bf16[16,32,512]{2,1,0:T(8,128)(2,1)} %bitcast.5), calls=%async_computation.1 | async-start | bytes 1048576 | tf_op jit(solution)/shard_map/all_to_all | solution.py:107
  59.5 17.5 %all-to-all-done.1 = bf16[16,32,512]{2,1,0:T(8,128)(2,1)S(1)} async-done(((bf16[16,32,512]{2,1,0:T(8,128)(2,1)}), bf16[16,32,512]{2,1,0:T(8,128)(2,1)S(1)}, u32[]{:S(2)}, u32[]{:S(2)}) %all-to-all-start.1) | async-done | bytes 524320 | tf_op jit(solution)/shard_map/all_to_all | solution.py:107
  77.1 23.2 %all_to_all.39 = bf16[16,32,512]{2,1,0:T(8,128)(2,1)S(1)} all-to-all(bf16[16,32,512]{2,1,0:T(8,128)(2,1)S(1)} %broadcast_in_dim.15), channel_id=1, replica_groups=mesh['pair'=32,'col'=16] {'col'}, dimensions={0} | all-to-all | bytes 1048576 | tf_op jit(solution)/shard_map/all_to_all | solution.py:102
  100.3 0.0 copy-start.1
  100.3 0.2 copy.17
  100.5 1.4 fusion.14
  101.9 7.2 %all-to-all-start.3 = ((f32[32,16,512]{2,1,0:T(8,128)}), f32[32,16,512]{2,1,0:T(8,128)S(1)}, u32[]{:S(2)}, u32[]{:S(2)}) async-start(f32[32,16,512]{2,1,0:T(8,128)} %fusion.14), calls=%async_computation.3 | async-start | bytes 2097152 | tf_op jit(solution)/shard_map/all_to_all | solution.py:107
  109.1 0.0 copy-done.3
  109.1 0.0 copy-done.1
  109.1 1.7 convolution_convert_fusion
  110.8 26.2 %all-to-all-done.3 = f32[32,16,512]{2,1,0:T(8,128)S(1)} async-done(((f32[32,16,512]{2,1,0:T(8,128)}), f32[32,16,512]{2,1,0:T(8,128)S(1)}, u32[]{:S(2)}, u32[]{:S(2)}) %all-to-all-start.3) | async-done | bytes 1048608 | tf_op jit(solution)/shard_map/all_to_all | solution.py:107
  137.1 3.9 %all-to-all-start.5 = ((bf16[32,32,512]{2,1,0:T(8,128)(2,1)}), bf16[32,32,512]{2,1,0:T(8,128)(2,1)S(1)}, u32[]{:S(2)}, u32[]{:S(2)}) async-start(bf16[32,32,512]{2,1,0:T(8,128)(2,1)} %bitcast.57), calls=%async_computation.5 | async-start | bytes 2097152 | tf_op jit(solution)/shard_map/all_to_all | solution.py:107
  141.0 0.1 reduce_sum.21
  141.0 27.9 %all-to-all-done.5 = bf16[32,32,512]{2,1,0:T(8,128)(2,1)S(1)} async-done(((bf16[32,32,512]{2,1,0:T(8,128)(2,1)}), bf16[32,32,512]{2,1,0:T(8,128)(2,1)S(1)}, u32[]{:S(2)}, u32[]{:S(2)}) %all-to-all-start.5) | async-done | bytes 1048608 | tf_op jit(solution)/shard_map/all_to_all | solution.py:107
  168.9 1.1 broadcast_in_dim.16
  170.0 3.9 %all-to-all-start.4 = ((f32[32,16,512]{2,1,0:T(8,128)}), f32[32,16,512]{2,1,0:T(8,128)S(1)}, u32[]{:S(2)}, u32[]{:S(2)}) async-start(f32[32,16,512]{2,1,0:T(8,128)} %broadcast_in_dim.16), calls=%async_computation.4 | async-start | bytes 2097152 | tf_op jit(solution)/shard_map/all_to_all | solution.py:102
  174.0 0.2 reduce_sum.22
  174.1 27.8 %all-to-all-done.4 = f32[32,16,512]{2,1,0:T(8,128)S(1)} async-done(((f32[32,16,512]{2,1,0:T(8,128)}), f32[32,16,512]{2,1,0:T(8,128)S(1)}, u32[]{:S(2)}, u32[]{:S(2)}) %all-to-all-start.4) | async-done | bytes 1048608 | tf_op jit(solution)/shard_map/all_to_all | solution.py:102
  201.9 1.1 broadcast_in_dim.17
  203.0 3.9 %all-to-all-start.6 = ((bf16[32,32,512]{2,1,0:T(8,128)(2,1)}), bf16[32,32,512]{2,1,0:T(8,128)(2,1)S(1)}, u32[]{:S(2)}, u32[]{:S(2)}) async-start(bf16[32,32,512]{2,1,0:T(8,128)(2,1)} %broadcast_in_dim.17), calls=%async_computation.6 | async-start | bytes 2097152 | tf_op jit(solution)/shard_map/all_to_all | solution.py:102
  207.0 24.3 %panel_factor.1 = (f32[512,512]{1,0:T(8,128)}, f32[512,512]{1,0:T(8,128)S(1)}) custom-call(f32[512,512]{1,0:T(8,128)S(1)} %bitcast.43), custom_call_target="tpu_custom_call" | custom-call | flops 536870912 | bytes 3145728 | tf_op jit(solution)/shard_map/panel_factor/pallas_call | solution.py:88
  231.3 2.5 %fusion.12 = f32[512,512]{1,0:T(8,128)} fusion(bf16[512,512]{1,0:T(8,128)(2,1)} %bitcast.49, f32[512,512]{1,0:T(8,128)S(1)} %get-tuple-element.4), kind=kOutput, calls=%fused_computation.29 | convolution fusion | flops 268697600 | bytes 2621440 | tf_op jit(solution)/shard_map/dot_general | solution.py:152
  233.8 1.1 all-to-all-done.6
  234.9 0.7 fusion.10
  235.7 0.0 copy-start.2
  235.7 1.7 add_convert_fusion
  237.4 0.0 copy-done.2
  237.4 2.9 %fusion.2 = bf16[64,8,8,128]{3,1,2,0:T(8,128)(2,1)S(1)} fusion(bf16[1024,512]{1,0:T(8,128)(2,1)} %add_convert_fusion, pred[1024]{0:T(1024)(128)(4,1)S(1)} %fusion.6, f32[512,512]{1,0:T(8,128)} %fusion.12, bf16[512,512]{1,0:T(8,128)(2,1)S(1)} %bitcast.50, f32[512,512]{1,0:T(8,128)S(1)} %get-tuple-element.4, bf16[64,8,8,128]{3,2,1,0:T(8,128)(2,1)} %bitcast.54), kind=kOutput, calls=%fused_computation.7 | convolution fusion | flops 808976384 | bytes 5768192 | tf_op jit(solution)/shard_map/dot_general | solution.py:160
  240.3 1.2 copy.19
  (5 shorter events, 0.1 us)
Async XLA Ops:
  0.6 15.0 %copy-start = (f32[128,128]{1,0:T(8,128)S(1)}, f32[128,128]{1,0:T(8,128)}, u32[]{:S(2)}) copy-start(f32[128,128]{1,0:T(8,128)} %param.4) | copy-start | bytes 196612
  3.6 39.3 %all-to-all-start = ((bf16[4,128,8,128]{1,2,0,3:T(8,128)(2,1)}), bf16[4,128,8,128]{1,2,0,3:T(8,128)(2,1)S(1)}, u32[]{:S(2)}, u32[]{:S(2)}) async-start(bf16[4,128,8,128]{1,2,0,3:T(8,128)(2,1)} %copy.13), calls=%async_computation | async-start | bytes 2097152 | tf_op jit(solution)/shard_map/all_to_all | solution.py:129
  45.7 63.4 %copy-start.3 = (bf16[4,128,8,128]{3,2,1,0:T(8,128)(2,1)}, bf16[4,128,8,128]{3,2,1,0:T(8,128)(2,1)S(1)}, u32[]{:S(2)}) copy-start(bf16[4,128,8,128]{3,2,1,0:T(8,128)(2,1)S(1)} %copy.16) | copy-start | bytes 3145732
  46.8 30.2 %all-to-all-start.1 = ((bf16[16,32,512]{2,1,0:T(8,128)(2,1)}), bf16[16,32,512]{2,1,0:T(8,128)(2,1)S(1)}, u32[]{:S(2)}, u32[]{:S(2)}) async-start(bf16[16,32,512]{2,1,0:T(8,128)(2,1)} %bitcast.5), calls=%async_computation.1 | async-start | bytes 1048576 | tf_op jit(solution)/shard_map/all_to_all | solution.py:107
  100.3 8.8 %copy-start.1 = (bf16[16,32,512]{2,1,0:T(8,128)(2,1)}, bf16[16,32,512]{2,1,0:T(8,128)(2,1)S(1)}, u32[]{:S(2)}) copy-start(bf16[16,32,512]{2,1,0:T(8,128)(2,1)S(1)} %all_to_all.39) | copy-start | bytes 1572868
  101.9 35.1 %all-to-all-start.3 = ((f32[32,16,512]{2,1,0:T(8,128)}), f32[32,16,512]{2,1,0:T(8,128)S(1)}, u32[]{:S(2)}, u32[]{:S(2)}) async-start(f32[32,16,512]{2,1,0:T(8,128)} %fusion.14), calls=%async_computation.3 | async-start | bytes 2097152 | tf_op jit(solution)/shard_map/all_to_all | solution.py:107
  137.1 31.9 %all-to-all-start.5 = ((bf16[32,32,512]{2,1,0:T(8,128)(2,1)}), bf16[32,32,512]{2,1,0:T(8,128)(2,1)S(1)}, u32[]{:S(2)}, u32[]{:S(2)}) async-start(bf16[32,32,512]{2,1,0:T(8,128)(2,1)} %bitcast.57), calls=%async_computation.5 | async-start | bytes 2097152 | tf_op jit(solution)/shard_map/all_to_all | solution.py:107
  170.0 31.9 %all-to-all-start.4 = ((f32[32,16,512]{2,1,0:T(8,128)}), f32[32,16,512]{2,1,0:T(8,128)S(1)}, u32[]{:S(2)}, u32[]{:S(2)}) async-start(f32[32,16,512]{2,1,0:T(8,128)} %broadcast_in_dim.16), calls=%async_computation.4 | async-start | bytes 2097152 | tf_op jit(solution)/shard_map/all_to_all | solution.py:102
  203.0 31.9 %all-to-all-start.6 = ((bf16[32,32,512]{2,1,0:T(8,128)(2,1)}), bf16[32,32,512]{2,1,0:T(8,128)(2,1)S(1)}, u32[]{:S(2)}, u32[]{:S(2)}) async-start(bf16[32,32,512]{2,1,0:T(8,128)(2,1)} %broadcast_in_dim.17), calls=%async_computation.6 | async-start | bytes 2097152 | tf_op jit(solution)/shard_map/all_to_all | solution.py:102
  235.7 1.7 copy-start.2

commit v2 on v1

--- a/solution.py
+++ b/solution.py
@@ -11,6 +11,8 @@
 BLOCK = 128
 STRIP = 4
 EXACT = lax.Precision.HIGHEST
+MESH = pl.DeviceIdType.MESH
+Y = 8
 
 
 def factor_block(work):
@@ -97,14 +99,227 @@
     )(gram)
 
 
+def exchange_kernel(owner_ref, cand_ref, tile_ref, panel_ref, gram_ref, mine_ref,
+                    picks, gpart, gin, spart, score, shalf, sin,
+                    p_send, p_recv, q_send, q_recv, g1_send, g1_recv, g2_send, g2_recv,
+                    g3_send, g3_recv, g4_send, g4_recv, s1_send, s1_recv, s2_send, s2_recv):
+    pair = lax.axis_index("pair")
+    colm = lax.axis_index("col")
+    n_pair = lax.axis_size("pair")
+    n_chip = n_pair // 2
+    chip, core = pair // 2, lax.rem(pair, 2)
+    half, y = colm // Y, lax.rem(colm, Y)
+    other_core = 2 * chip + 1 - core
+    part = cand_ref.shape[0] // Y
+    width = cand_ref.shape[1]
+
+    barrier = pltpu.get_barrier_semaphore()
+
+    def greet_pair(d, carry):
+        pl.semaphore_signal(barrier, inc=1, device_id={"pair": lax.rem(pair + d, n_pair)}, device_id_type=MESH)
+        return carry
+
+    def greet_y(d, carry):
+        pl.semaphore_signal(barrier, inc=1, device_id={"col": half * Y + lax.rem(y + d, Y)}, device_id_type=MESH)
+        return carry
+
+    lax.fori_loop(1, n_pair, greet_pair, 0)
+    lax.fori_loop(1, Y, greet_y, 0)
+    pl.semaphore_signal(barrier, inc=1, device_id={"col": (1 - half) * Y + y}, device_id_type=MESH)
+    pl.semaphore_wait(barrier, n_pair + Y - 1)
+
+    def rows_of(ref, k):
+        return ref.at[pl.ds(pl.multiple_of(k * part, part), part)]
+
+    def offer(k):
+        return pltpu.make_async_remote_copy(
+            src_ref=rows_of(cand_ref, k), dst_ref=picks.at[y], send_sem=p_send.at[k], recv_sem=p_recv.at[y],
+            device_id={"col": k}, device_id_type=MESH)
+
+    def offered(k):
+        return pltpu.make_async_remote_copy(
+            src_ref=rows_of(cand_ref, k), dst_ref=picks.at[k], send_sem=p_send.at[k], recv_sem=p_recv.at[k],
+            device_id={"col": k}, device_id_type=MESH)
+
+    def across():
+        return pltpu.make_async_remote_copy(
+            src_ref=rows_of(panel_ref, y), dst_ref=rows_of(panel_ref, y), send_sem=q_send.at[0], recv_sem=q_recv.at[0],
+            device_id={"col": (1 - half) * Y + y}, device_id_type=MESH)
+
+    def gather(k):
+        return pltpu.make_async_remote_copy(
+            src_ref=rows_of(panel_ref, y), dst_ref=rows_of(panel_ref, y), send_sem=g2_send.at[0, k], recv_sem=g2_recv.at[0, y],
+            device_id={"col": half * Y + k}, device_id_type=MESH)
+
+    def gathered(k):
+        return pltpu.make_async_remote_copy(
+            src_ref=rows_of(panel_ref, y), dst_ref=rows_of(panel_ref, k), send_sem=g2_send.at[0, k], recv_sem=g2_recv.at[0, k],
+            device_id={"col": half * Y + k}, device_id_type=MESH)
+
+    @pl.when(half == 0)
+    def _():
+        lax.fori_loop(1, Y, lambda d, c: (offer(lax.rem(y + d, Y)).start(), c)[1], 0)
+        picks[y] = cand_ref[pl.ds(pl.multiple_of(y * part, part), part), :]
+        lax.fori_loop(1, Y, lambda d, c: (offered(lax.rem(y + d, Y)).wait_recv(), c)[1], 0)
+        panel_ref[pl.ds(pl.multiple_of(y * part, part), part), :] = picks[owner_ref[0]]
+        across().start()
+
+    @pl.when(half == 1)
+    def _():
+        across().wait_recv()
+
+    lax.fori_loop(1, Y, lambda d, c: (gather(lax.rem(y + d, Y)).start(), c)[1], 0)
+    lax.fori_loop(1, Y, lambda d, c: (gathered(lax.rem(y + d, Y)).wait_recv(), c)[1], 0)
+
+    over_rows = (((0,), (0,)), ((), ()))
+    lead = pl.multiple_of((y // 2) * BLOCK, BLOCK)
+    gpart[...] = lax.dot_general(panel_ref[:, pl.ds(lead, BLOCK)], panel_ref[...], over_rows,
+                                 preferred_element_type=jnp.float32)
+    base = lax.rem(y, 2) * part
+    wide = width // BLOCK
+
+    def piece(i):
+        return gpart.at[pl.ds(pl.multiple_of(base + (i // wide) * 8, 8), 8),
+                        pl.ds(pl.multiple_of(lax.rem(i, wide) * BLOCK, BLOCK), BLOCK)]
+
+    def g1(i, slot):
+        return pltpu.make_async_remote_copy(
+            src_ref=piece(i), dst_ref=gin.at[slot], send_sem=g1_send.at[i], recv_sem=g1_recv.at[slot],
+            device_id={"pair": i}, device_id_type=MESH)
+
+    lax.fori_loop(1, n_pair, lambda d, c: (g1(lax.rem(pair + d, n_pair), pair).start(), c)[1], 0)
+    gin[pair] = gpart[pl.ds(pl.multiple_of(base + (pair // wide) * 8, 8), 8),
+                      pl.ds(pl.multiple_of(lax.rem(pair, wide) * BLOCK, BLOCK), BLOCK)]
+
+    def products(k, c):
+        lane = pl.multiple_of(k * 2 * BLOCK, 2 * BLOCK)
+        out = lax.dot_general(tile_ref[:, pl.ds(lane, 2 * BLOCK)], panel_ref[...], over_rows,
+                              preferred_element_type=jnp.float32).astype(jnp.bfloat16)
+        count = 2 * BLOCK // (2 * chunk)
+        spart[pl.ds(k * count, count)] = out.reshape(count, 2, chunk, width)
+        return c
+
+    chunk = tile_ref.shape[1] // n_pair
+    lax.fori_loop(0, tile_ref.shape[1] // (2 * BLOCK), products, 0)
+
+    def s1():
+        return pltpu.make_async_remote_copy(
+            src_ref=spart.at[:, 1 - core], dst_ref=score, send_sem=s1_send.at[0], recv_sem=s1_recv.at[0],
+            device_id={"pair": other_core}, device_id_type=MESH)
+
+    s1().start()
+
+    lax.fori_loop(1, n_pair, lambda d, c: (g1(lax.rem(pair + d, n_pair), lax.rem(pair + d, n_pair)).wait_recv(), c)[1], 0)
+    my_r, my_c = pair // wide, lax.rem(pair, wide)
+
+    def column(ref_c):
+        return pl.ds(pl.multiple_of(ref_c * BLOCK, BLOCK), BLOCK)
+
+    gram_ref[y, my_r, :, column(my_c)] = jnp.sum(gin[...], axis=0)
+
+    def g2(k, row):
+        where = gram_ref.at[row, my_r, :, column(my_c)]
+        return pltpu.make_async_remote_copy(
+            src_ref=where, dst_ref=where, send_sem=g2_send.at[1, k], recv_sem=g2_recv.at[1, row],
+            device_id={"col": half * Y + k}, device_id_type=MESH)
+
+    lax.fori_loop(1, Y, lambda d, c: (g2(lax.rem(y + d, Y), y).start(), c)[1], 0)
+    lax.fori_loop(1, Y, lambda d, c: (g2(lax.rem(y + d, Y), lax.rem(y + d, Y)).wait_recv(), c)[1], 0)
+
+    def g3(t, source):
+        where = gram_ref.at[:, source // wide, :, column(lax.rem(source, wide))]
+        return pltpu.make_async_remote_copy(
+            src_ref=where, dst_ref=where, send_sem=g3_send.at[t], recv_sem=g3_recv.at[source // 2],
+            device_id={"pair": 2 * t + core}, device_id_type=MESH)
+
+    def g4(source):
+        where = gram_ref.at[:, source // wide, :, column(lax.rem(source, wide))]
+        return pltpu.make_async_remote_copy(
+            src_ref=where, dst_ref=where, send_sem=g4_send.at[source // 2], recv_sem=g4_recv.at[source // 2],
+            device_id={"pair": other_core}, device_id_type=MESH)
+
+    lax.fori_loop(1, n_chip, lambda d, c: (g3(lax.rem(chip + d, n_chip), pair).start(), c)[1], 0)
+    g4(pair).start()
+
+    s1().wait_recv()
+
+    def add_cores(k, c):
+        shalf[k] = (spart[k, core].astype(jnp.float32) + score[k].astype(jnp.float32)).astype(jnp.bfloat16)
+        return c
+
+    lax.fori_loop(0, n_chip, add_cores, 0)
+
+    def s2(t, slot):
+        return pltpu.make_async_remote_copy(
+            src_ref=shalf.at[t], dst_ref=sin.at[slot], send_sem=s2_send.at[t], recv_sem=s2_recv.at[slot],
+            device_id={"pair": 2 * t + core}, device_id_type=MESH)
+
+    lax.fori_loop(1, n_chip, lambda d, c: (s2(lax.rem(chip + d, n_chip), chip).start(), c)[1], 0)
+    sin[chip] = shalf[chip]
+
+    def forward(d, c):
+        t = lax.rem(chip + n_chip - d, n_chip)
+        g3(t, 2 * t + core).wait_recv()
+        g4(2 * t + core).start()
+        return c
+
+    lax.fori_loop(1, n_chip, forward, 0)
+    lax.fori_loop(1, n_chip, lambda d, c: (s2(lax.rem(chip + d, n_chip), lax.rem(chip + d, n_chip)).wait_recv(), c)[1], 0)
+    mine_ref[...] = jnp.sum(sin[...].astype(jnp.float32), axis=0).astype(jnp.bfloat16)
+    lax.fori_loop(0, n_chip, lambda t, c: (g4(2 * t + 1 - core).wait_recv(), c)[1], 0)
+
+    @pl.when(half == 0)
+    def _():
+        lax.fori_loop(1, Y, lambda d, c: (offer(lax.rem(y + d, Y)).wait_send(), c)[1], 0)
+        across().wait_send()
+
+    lax.fori_loop(1, Y, lambda d, c: (gather(lax.rem(y + d, Y)).wait_send(), c)[1], 0)
+    lax.fori_loop(1, Y, lambda d, c: (g2(lax.rem(y + d, Y), y).wait_send(), c)[1], 0)
+    lax.fori_loop(1, n_pair, lambda d, c: (g1(lax.rem(pair + d, n_pair), pair).wait_send(), c)[1], 0)
+    s1().wait_send()
+    lax.fori_loop(1, n_chip, lambda d, c: (g3(lax.rem(chip + d, n_chip), pair).wait_send(), c)[1], 0)
+    lax.fori_loop(1, n_chip, lambda d, c: (s2(lax.rem(chip + d, n_chip), chip).wait_send(), c)[1], 0)
+    lax.fori_loop(0, n_chip, lambda t, c: (g4(2 * t + core).wait_send(), c)[1], 0)
+
+
+def exchange(owner, cand, tile):
+    rows, width = cand.shape
+    n_pair = lax.axis_size("pair")
+    n_chip = n_pair // 2
+    chunk = tile.shape[1] // n_pair
+    vmem = pl.BlockSpec(memory_space=pltpu.VMEM)
+    dma = pltpu.SemaphoreType.DMA
+    f32, bf16 = jnp.float32, jnp.bfloat16
+    sems = []
+    for shape in ((Y,), (1,), (n_pair,), (2, Y), (n_chip,), (n_chip,), (1,), (n_chip,)):
+        sems += [dma(shape), dma(shape)]
+    return pl.pallas_call(
+        exchange_kernel,
+        out_shape=(
+            jax.ShapeDtypeStruct((rows, width), bf16),
+            jax.ShapeDtypeStruct((Y, width // Y // 8, 8, width), f32),
+            jax.ShapeDtypeStruct((chunk, width), bf16),
+        ),
+        in_specs=[pl.BlockSpec(memory_space=pltpu.SMEM), vmem, vmem],
+        out_specs=(vmem,) * 3,
+        scratch_shapes=[
+            pltpu.VMEM((Y, rows // Y, width), bf16),
+            pltpu.VMEM((BLOCK, width), f32),
+            pltpu.VMEM((n_pair, 8, BLOCK), f32),
+            pltpu.VMEM((n_chip, 2, chunk, width), bf16),
+            pltpu.VMEM((n_chip, chunk, width), bf16),
+            pltpu.VMEM((n_chip, chunk, width), bf16),
+            pltpu.VMEM((n_chip, chunk, width), bf16),
+            *sems,
+        ],
+        compiler_params=pltpu.CompilerParams(collective_id=0, has_side_effects=True, vmem_limit_bytes=32 << 20),
+        name="panel_exchange",
+    )(owner, cand, tile)
+
+
 def share(value, axis):
     count = lax.axis_size(axis)
     return lax.all_to_all(jnp.broadcast_to(value[None], (count, *value.shape)), axis, 0, 0)
-
-
-def collect(value, axis):
-    count = lax.axis_size(axis)
-    return lax.all_to_all(value.reshape(count, value.shape[0] // count, *value.shape[1:]), axis, 0, 0)
 
 
 def build_block(moved, s_index, one_cols):
@@ -133,15 +348,8 @@
     owner_col = first_orb // r_count
     within = first_orb % r_count
     panel_cols = lax.dynamic_slice_in_dim(local_tile, within * orbitals, panel_width, 1)
-    mine = lax.dynamic_index_in_dim(collect(panel_cols, "col"), owner_col, 0, keepdims=False)
-    panel = share(mine, "col").reshape(row_count, panel_width)
-    gram_part = lax.dot_general(panel, panel, (((0,), (0,)), ((), ())), preferred_element_type=jnp.float32)
-    gram = share(collect(gram_part, "pair").sum(0), "pair").reshape(panel_width, panel_width)
-    triangle, inverse = factor(gram, orbitals)
-    sums_part = lax.dot_general(
-        local_tile, panel, (((0,), (0,)), ((), ())), preferred_element_type=jnp.float32
-    ).astype(jnp.bfloat16)
-    sums_mine = collect(sums_part, "pair").astype(jnp.float32).sum(0).astype(jnp.bfloat16)
+    panel, gram, sums_mine = exchange(owner_col[None], panel_cols, local_tile)
+    triangle, inverse = factor(gram.reshape(panel_width, panel_width), orbitals)
     sums_t = share(sums_mine, "pair").reshape(col_count, panel_width)
     inverse_hi = inverse.astype(jnp.bfloat16)
     inverse_lo = (inverse - inverse_hi.astype(jnp.float32)).astype(jnp.bfloat16)

time: 242 us -> 168 us (0.69)
  waiting for transfers between devices: 128 us -> 29.1 us
  Pallas kernels: 24.3 us -> 98.4 us
  starting transfers between devices: 42.9 us -> 18.4 us
  blocking collectives: 23.2 us -> 0 us
    pallas_call x0 -> x1, Pallas kernels: none -> 74 us  [exchange(): pl.pallas_call(exchange_kernel, out_shape=(jax.ShapeDtypeStruct((rows, wi...]
    all_to_all x3 -> x0, waiting for transfers between devices: 71.7 us -> none  [collect(): lax.all_to_all(value.reshape(count, value.shape[0] // count, *value.shape...]
    all_to_all x2 -> x1, waiting for transfers between devices: 28.9 us -> 2.07 us  [share(): lax.all_to_all(jnp.broadcast_to(value[None], (count, *value.shape)), axis...]
    all_to_all x3 -> x0, starting transfers between devices: 23.7 us -> none  [collect(): lax.all_to_all(value.reshape(count, value.shape[0] // count, *value.shape...]
    all_to_all x1 -> x0, blocking collectives: 23.2 us -> none  [share(): lax.all_to_all(jnp.broadcast_to(value[None], (count, *value.shape)), axis...]
    dot_general x2 -> x0, matrix products: 3.13 us -> none  [the longest x1 1.72 us: per_device(): lax.dot_general(local_tile, panel, (((0,), (0,)), ((), ())), preferred_el...]
    unnamed x11 -> x9, local copies, waits for them, and re-layouts: 4.47 us -> 5.69 us
    all_to_all x2 -> x1, starting transfers between devices: 7.82 us -> 7.01 us  [share(): lax.all_to_all(jnp.broadcast_to(value[None], (count, *value.shape)), axis...]
  transfers between devices with their start and end apart: 6 -> 2, of which waited for: 6 -> 2; matrix products, arithmetic and copies ran while one was open for 2% -> 1% of each run, Pallas kernels for 10% -> 15%
where the time goes in v2:
time: 168 us; the launch traced here: 167 us
  Pallas kernels  98.4 us (59%)
  waiting for transfers between devices  29.1 us (17%)
  starting transfers between devices  18.4 us (11%)
  matrix products  10 us (6%)
  local copies, waits for them, and re-layouts  8.61 us (5%)
    pallas_call x1, Pallas kernels, exchange(): pl.pallas_call(exchange_kernel, out_shape=(jax.ShapeDtypeStruct((rows, wi...  74 us
    all_to_all x1, waiting for transfers between devices, per_device(): lax.all_to_all(two_rdm, 'pair', split_axis=3, concat_axis=0, tiled=True)  27 us
    pallas_call x1, Pallas kernels, factor(): pl.pallas_call(functools.partial(factor_kernel, scale), out_shape=(jax.Sh...  24.3 us
    all_to_all x1, starting transfers between devices, per_device(): lax.all_to_all(two_rdm, 'pair', split_axis=3, concat_axis=0, tiled=True)  11.4 us
    all_to_all x1, starting transfers between devices, share(): lax.all_to_all(jnp.broadcast_to(value[None], (count, *value.shape)), axis...  7.01 us
    unnamed x9, local copies, waits for them, and re-layouts  5.69 us
    dot_general x1, matrix products, per_device(): lax.dot_general(basis, weights_t, (((1,), (1,)), ((), ())), preferred_ele...  3.54 us
    dot_general x2, matrix products, solve_right(): lax.dot_general(value, inverse_hi, dims, preferred_element_type=jnp.float32)  3.46 us
  transfers between devices with their start and end apart: 2, of which 2 were waited for; matrix products, arithmetic and copies ran while one was open for 1% of the time, Pallas kernels for 15%

profile of v2, /device:TPU:1, one launch (start us, length us, event | category | flops | bytes accessed | tf_op | source)
XLA Modules:
  0.0 167.1 jit_solution(6566598575204413765)
XLA Ops:
  0.6 0.0 copy-start
  0.6 2.9 %copy.11 = bf16[4,128,8,128]{1,2,0,3:T(8,128)(2,1)} copy(bf16[4,128,8,128]{3,2,1,0:T(8,128)(2,1)} %param.3) | data formatting | bytes 2097152 | tf_op args[0]
  3.6 11.4 %all-to-all-start = ((bf16[4,128,8,128]{1,2,0,3:T(8,128)(2,1)}), bf16[4,128,8,128]{1,2,0,3:T(8,128)(2,1)S(1)}, u32[]{:S(2)}, u32[]{:S(2)}) async-start(bf16[4,128,8,128]{1,2,0,3:T(8,128)(2,1)} %copy.11), calls=%async_computation | async-start | bytes 2097152 | tf_op jit(solution)/shard_map/all_to_all | solution.py:344
  15.7 0.0 copy-done
  15.7 0.1 constant_dynamic-slice_fusion.1
  15.7 0.1 copy.10
  15.8 27.0 %all-to-all-done = bf16[4,128,8,128]{1,2,0,3:T(8,128)(2,1)S(1)} async-done(((bf16[4,128,8,128]{1,2,0,3:T(8,128)(2,1)}), bf16[4,128,8,128]{1,2,0,3:T(8,128)(2,1)S(1)}, u32[]{:S(2)}, u32[]{:S(2)}) %all-to-all-start) | async-done | bytes 1048608 | tf_op jit(solution)/shard_map/all_to_all | solution.py:344
  42.8 0.2 copy.12
  43.0 0.3 convert_bitcast_fusion
  43.3 0.2 copy.13
  43.6 0.9 fusion.1
  44.4 1.2 copy.14
  45.7 0.0 copy-start.1
  45.7 0.3 copy.20
  46.0 74.0 %panel_exchange.1 = (bf16[512,512]{1,0:T(8,128)(2,1)S(1)}, f32[8,8,8,512]{3,2,1,0:T(8,128)S(1)}, bf16[32,512]{1,0:T(8,128)(2,1)S(1)}) custom-call(s32[1]{0:T(128)} %bitcast.5.owner_ref, bf16[512,512]{1,0:T(8,128)(2,1)S(1)} %constant_dynamic-slice_fusion.cand_ref, bf16[512,1024]{1,0:T(8,128)(2,1)S(1)} %bitcast.31), custom_call_target="tpu_custom_call" | custom-call | tf_op jit(solution)/shard_map/panel_exchange/pallas_call | solution.py:296
  120.1 0.0 copy-done.1
  120.1 1.1 broadcast_in_dim.11
  121.2 7.0 %all-to-all-start.1 = ((bf16[32,32,512]{2,1,0:T(8,128)(2,1)}), bf16[32,32,512]{2,1,0:T(8,128)(2,1)}, u32[]{:S(2)}, u32[]{:S(2)}) async-start(bf16[32,32,512]{2,1,0:T(8,128)(2,1)} %broadcast_in_dim.11), calls=%async_computation.1 | async-start | bytes 2097152 | tf_op jit(solution)/shard_map/all_to_all | solution.py:322
  128.2 24.3 %panel_factor.1 = (f32[512,512]{1,0:T(8,128)}, f32[512,512]{1,0:T(8,128)S(1)}) custom-call(f32[512,512]{1,0:T(8,128)S(1)} %bitcast.32), custom_call_target="tpu_custom_call" | custom-call | flops 536870912 | bytes 3145728 | tf_op jit(solution)/shard_map/panel_factor/pallas_call | solution.py:90
  152.5 1.5 fusion.12
  154.0 2.1 %all-to-all-done.1 = bf16[32,32,512]{2,1,0:T(8,128)(2,1)} async-done(((bf16[32,32,512]{2,1,0:T(8,128)(2,1)}), bf16[32,32,512]{2,1,0:T(8,128)(2,1)}, u32[]{:S(2)}, u32[]{:S(2)}) %all-to-all-start.1) | async-done | bytes 1048608 | tf_op jit(solution)/shard_map/all_to_all | solution.py:322
  156.1 2.0 %fusion.10 = f32[1024,512]{1,0:T(8,128)S(1)} fusion(bf16[1024,512]{1,0:T(8,128)(2,1)} %bitcast.7, f32[512,512]{1,0:T(8,128)S(1)} %get-tuple-element.9), kind=kOutput, calls=%fused_computation.25 | convolution fusion | flops 537133056 | bytes 4194304 | tf_op jit(solution)/shard_map/dot_general | solution.py:360
  158.1 0.0 copy-start.2
  158.1 3.0 %add_convert_fusion = bf16[1024,512]{1,0:T(8,128)(2,1)} fusion(f32[1024,512]{1,0:T(8,128)S(1)} %fusion.10, bf16[1024,512]{1,0:T(8,128)(2,1)} %bitcast.7, f32[512,512]{1,0:T(8,128)S(1)} %get-tuple-element.9), kind=kOutput, calls=%fused_computation.5 | convolution fusion | flops 538968064 | bytes 5242880 | tf_op jit(solution)/shard_map/dot_general | solution.py:361
  161.1 0.0 copy-done.2
  161.1 3.5 %fusion.2 = bf16[64,8,8,128]{3,1,2,0:T(8,128)(2,1)} fusion(bf16[1024,512]{1,0:T(8,128)(2,1)} %add_convert_fusion, pred[1024]{0:T(1024)(128)(4,1)S(1)} %fusion.6, f32[512,512]{1,0:T(8,128)} %fusion.12, bf16[512,512]{1,0:T(8,128)(2,1)S(1)} %get-tuple-element.7, f32[512,512]{1,0:T(8,128)S(1)} %get-tuple-element.9, bf16[64,8,8,128]{3,2,1,0:T(8,128)(2,1)S(1)} %bitcast.35), kind=kOutput, calls=%fused_computation.6 | convolution fusion | flops 808976384 | bytes 5768192 | tf_op jit(solution)/shard_map/dot_general | solution.py:368
  164.7 2.5 %copy.16 = bf16[64,8,8,128]{3,2,1,0:T(8,128)(2,1)} copy(bf16[64,8,8,128]{3,1,2,0:T(8,128)(2,1)} %fusion.2) | data formatting | bytes 2097152
  (4 shorter events, 0.1 us)
Async XLA Ops:
  0.6 15.0 %copy-start = (f32[128,128]{1,0:T(8,128)S(1)}, f32[128,128]{1,0:T(8,128)}, u32[]{:S(2)}) copy-start(f32[128,128]{1,0:T(8,128)} %param.4) | copy-start | bytes 196612
  3.6 39.3 %all-to-all-start = ((bf16[4,128,8,128]{1,2,0,3:T(8,128)(2,1)}), bf16[4,128,8,128]{1,2,0,3:T(8,128)(2,1)S(1)}, u32[]{:S(2)}, u32[]{:S(2)}) async-start(bf16[4,128,8,128]{1,2,0,3:T(8,128)(2,1)} %copy.11), calls=%async_computation | async-start | bytes 2097152 | tf_op jit(solution)/shard_map/all_to_all | solution.py:344
  45.7 74.4 %copy-start.1 = (bf16[4,128,8,128]{3,2,1,0:T(8,128)(2,1)}, bf16[4,128,8,128]{3,2,1,0:T(8,128)(2,1)S(1)}, u32[]{:S(2)}) copy-start(bf16[4,128,8,128]{3,2,1,0:T(8,128)(2,1)S(1)} %copy.14) | copy-start | bytes 3145732
  121.2 34.9 %all-to-all-start.1 = ((bf16[32,32,512]{2,1,0:T(8,128)(2,1)}), bf16[32,32,512]{2,1,0:T(8,128)(2,1)}, u32[]{:S(2)}, u32[]{:S(2)}) async-start(bf16[32,32,512]{2,1,0:T(8,128)(2,1)} %broadcast_in_dim.11), calls=%async_computation.1 | async-start | bytes 2097152 | tf_op jit(solution)/shard_map/all_to_all | solution.py:322
  158.1 3.0 %copy-start.2 = (bf16[4,128,8,128]{3,2,1,0:T(8,128)(2,1)S(1)}, bf16[4,128,8,128]{3,2,1,0:T(8,128)(2,1)}, u32[]{:S(2)}) copy-start(bf16[4,128,8,128]{3,2,1,0:T(8,128)(2,1)} %copy-done.1) | copy-start | bytes 3145732

commit v3 on v1

--- a/solution.py
+++ b/solution.py
@@ -11,6 +11,9 @@
 BLOCK = 128
 STRIP = 4
 EXACT = lax.Precision.HIGHEST
+MESH = pl.DeviceIdType.MESH
+PIECES = 2
+Y = 8
 
 
 def factor_block(work):
@@ -97,23 +100,260 @@
     )(gram)
 
 
+def wrap(value, count):
+    return jnp.where(value >= count, value - count, value)
+
+
+def each(start, stop, body):
+    lax.fori_loop(start, stop, lambda k, c: (body(k), c)[1], 0)
+
+
+def exchange_kernel(owner_ref, x_ref, one_ref, panel_ref, gt_ref, gram_ref, mine_ref,
+                    land, order, picks_a, picks_b, gpart, gin, spart, score, shalf, sin,
+                    a_send, a_recv, p_send, p_recv, q_send, q_recv, c_send, c_recv, g1_send, g1_recv, g2_send, g2_recv,
+                    g3_send, g3_recv, g4_send, g4_recv, s1_send, s1_recv, s2_send, s2_recv):
+    pair = lax.axis_index("pair")
+    colm = lax.axis_index("col")
+    n_pair = lax.axis_size("pair")
+    n_chip = n_pair // 2
+    chip, core = pair // 2, lax.rem(pair, 2)
+    half, y = colm // Y, lax.rem(colm, Y)
+    other_core = 2 * chip + 1 - core
+    width = panel_ref.shape[0]
+    part = width // Y
+    wide = width // BLOCK
+    s_count = x_ref.shape[1]
+    s_piece = s_count // PIECES
+    over_last = (((1,), (1,)), ((), ()))
+    picks = (picks_a, picks_b)
+
+    def on_pair(src, dst, send, recv, k):
+        return pltpu.make_async_remote_copy(
+            src_ref=src, dst_ref=dst, send_sem=send, recv_sem=recv, device_id={"pair": k}, device_id_type=MESH)
+
+    def on_col(src, dst, send, recv, k):
+        return pltpu.make_async_remote_copy(
+            src_ref=src, dst_ref=dst, send_sem=send, recv_sem=recv, device_id={"col": k}, device_id_type=MESH)
+
+    barrier = pltpu.get_barrier_semaphore()
+    each(1, n_pair, lambda d: pl.semaphore_signal(
+        barrier, inc=1, device_id={"pair": wrap(pair + d, n_pair)}, device_id_type=MESH))
+    each(1, Y, lambda d: pl.semaphore_signal(
+        barrier, inc=1, device_id={"col": half * Y + wrap(y + d, Y)}, device_id_type=MESH))
+    pl.semaphore_signal(barrier, inc=1, device_id={"col": (1 - half) * Y + y}, device_id_type=MESH)
+    pl.semaphore_wait(barrier, n_pair + Y - 1)
+
+    def first(k, peer, slot):
+        ss = pl.ds(k * s_piece, s_piece)
+        return on_pair(x_ref.at[peer, ss, 0], land.at[0, slot, ss], a_send.at[k, peer], a_recv.at[k, slot], peer)
+
+    def second(peer, slot):
+        return on_pair(x_ref.at[peer, :, 1], land.at[1, slot], a_send.at[PIECES, peer], a_recv.at[PIECES, slot], peer)
+
+    for k in range(PIECES):
+        each(1, n_pair, lambda d: first(k, wrap(pair + d, n_pair), pair).start())
+    for h in range(2):
+        land[h, pair] = x_ref[pair, :, h]
+
+    row = lax.broadcasted_iota(jnp.int32, (width, width), 0)
+    col = lax.broadcasted_iota(jnp.int32, (width, width), 1)
+    q, r = row & (BLOCK - 1), row // BLOCK
+    order[...] = (col == (q // 4) * 16 + r * 4 + (q & 3)).astype(jnp.float32).astype(jnp.bfloat16)
+    q_row = lax.broadcasted_iota(jnp.int32, (BLOCK, BLOCK), 0)
+
+    def build(h, s):
+        moved = land[h, :, s].reshape(width, BLOCK)
+        placed = jnp.dot(order[...], moved, preferred_element_type=jnp.float32)
+        for r in range(wide):
+            diagonal = jnp.where(q_row == pair * s_count + s, one_ref[pl.ds(h * wide + r, 1), :], 0.0)
+            gt_ref[h, r * BLOCK:(r + 1) * BLOCK, s * BLOCK:(s + 1) * BLOCK] = (
+                diagonal - placed[r * BLOCK:(r + 1) * BLOCK]).astype(jnp.bfloat16)
+
+    span = s_piece * BLOCK
+
+    def block(k, piece):
+        return pl.ds(pl.multiple_of(k * part, part), part), pl.ds(piece * span, span)
+
+    def offer(piece, k, slot):
+        rows, lanes = block(k, piece)
+        return on_col(gt_ref.at[0, rows, lanes], picks[piece].at[slot], p_send.at[piece, k], p_recv.at[piece, slot], k)
+
+    def across(piece):
+        where = panel_ref.at[block(y, piece)]
+        return on_col(where, where, q_send.at[piece], q_recv.at[piece], (1 - half) * Y + y)
+
+    def gather(piece, k, row):
+        where = panel_ref.at[block(row, piece)]
+        return on_col(where, where, c_send.at[piece, k], c_recv.at[piece, row], half * Y + k)
+
+    for piece in range(PIECES):
+        each(1, n_pair, lambda d: first(piece, wrap(pair + d, n_pair), wrap(pair + d, n_pair)).wait_recv())
+        for s in range(piece * s_piece, (piece + 1) * s_piece):
+            build(0, s)
+
+        @pl.when(half == 0)
+        def _():
+            each(1, Y, lambda d: offer(piece, wrap(y + d, Y), y).start())
+            rows, lanes = block(y, piece)
+            picks[piece][y] = gt_ref[0, rows, lanes]
+
+    each(1, n_pair, lambda d: second(wrap(pair + d, n_pair), pair).start())
+
+    for piece in range(PIECES):
+        @pl.when(half == 0)
+        def _():
+            each(1, Y, lambda d: offer(piece, wrap(y + d, Y), wrap(y + d, Y)).wait_recv())
+            rows, lanes = block(y, piece)
+            panel_ref[rows, lanes] = picks[piece][owner_ref[0]]
+            across(piece).start()
+
+        @pl.when(half == 1)
+        def _():
+            across(piece).wait_recv()
+
+        each(1, Y, lambda d: gather(piece, wrap(y + d, Y), y).start())
+
+    each(1, n_pair, lambda d: second(wrap(pair + d, n_pair), wrap(pair + d, n_pair)).wait_recv())
+    for s in range(s_count):
+        build(1, s)
+    for piece in range(PIECES):
+        each(1, Y, lambda d: gather(piece, wrap(y + d, Y), wrap(y + d, Y)).wait_recv())
+
+    chunk = mine_ref.shape[0]
+    rows_at_once = 2 * BLOCK
+    count = rows_at_once // (2 * chunk)
+    for h in range(2):
+        for k in range(width // rows_at_once):
+            out = lax.dot_general(gt_ref[h, k * rows_at_once:(k + 1) * rows_at_once, :], panel_ref[...], over_last,
+                                  preferred_element_type=jnp.float32).astype(jnp.bfloat16)
+            at = (h * (width // rows_at_once) + k) * count
+            spart[at:at + count] = out.reshape(count, 2, chunk, width)
+
+    def s1():
+        return on_pair(spart.at[:, 1 - core], score, s1_send.at[0], s1_recv.at[0], other_core)
+
+    s1().start()
+
+    gpart[...] = lax.dot_general(panel_ref[pl.ds(pl.multiple_of(y * part, part), part), :], panel_ref[...], over_last,
+                                 preferred_element_type=jnp.float32)
+
+    def column(c):
+        return pl.ds(pl.multiple_of(c * BLOCK, BLOCK), BLOCK)
+
+    def g1(i, slot):
+        src = gpart.at[pl.ds(pl.multiple_of((i // wide) * 8, 8), 8), column(lax.rem(i, wide))]
+        return on_pair(src, gin.at[slot], g1_send.at[i], g1_recv.at[slot], i)
+
+    each(1, n_pair, lambda d: g1(wrap(pair + d, n_pair), pair).start())
+    my_r, my_c = pair // wide, lax.rem(pair, wide)
+    gin[pair] = gpart[pl.ds(pl.multiple_of(my_r * 8, 8), 8), column(my_c)]
+
+    s1().wait_recv()
+
+    def add_cores(k):
+        shalf[k] = (spart[k, core].astype(jnp.float32) + score[k].astype(jnp.float32)).astype(jnp.bfloat16)
+
+    each(0, n_chip, add_cores)
+
+    def s2(t, slot):
+        return on_pair(shalf.at[t], sin.at[slot], s2_send.at[t], s2_recv.at[slot], 2 * t + core)
+
+    each(1, n_chip, lambda d: s2(wrap(chip + d, n_chip), chip).start())
+    sin[chip] = shalf[chip]
+
+    each(1, n_pair, lambda d: g1(wrap(pair + d, n_pair), wrap(pair + d, n_pair)).wait_recv())
+    gram_ref[y, my_r, :, column(my_c)] = jnp.sum(gin[...], axis=0)
+
+    def g2(k, row):
+        where = gram_ref.at[row, my_r, :, column(my_c)]
+        return on_col(where, where, g2_send.at[k], g2_recv.at[row], half * Y + k)
+
+    each(1, Y, lambda d: g2(wrap(y + d, Y), y).start())
+    each(1, Y, lambda d: g2(wrap(y + d, Y), wrap(y + d, Y)).wait_recv())
+
+    def held(source):
+        return gram_ref.at[:, source // wide, :, column(lax.rem(source, wide))]
+
+    def g3(t, source):
+        return on_pair(held(source), held(source), g3_send.at[t], g3_recv.at[source // 2], 2 * t + core)
+
+    def g4(source):
+        return on_pair(held(source), held(source), g4_send.at[source // 2], g4_recv.at[source // 2], other_core)
+
+    each(1, n_chip, lambda d: g3(wrap(chip + d, n_chip), pair).start())
+    g4(pair).start()
+
+    each(1, n_chip, lambda d: s2(wrap(chip + d, n_chip), wrap(chip + d, n_chip)).wait_recv())
+    mine_ref[...] = jnp.sum(sin[...].astype(jnp.float32), axis=0).astype(jnp.bfloat16)
+
+    def forward(d):
+        source = 2 * wrap(chip + n_chip - d, n_chip) + core
+        g3(source // 2, source).wait_recv()
+        g4(source).start()
+
+    each(1, n_chip, forward)
+    each(0, n_chip, lambda t: g4(2 * t + 1 - core).wait_recv())
+
+    for k in range(PIECES):
+        each(1, n_pair, lambda d: first(k, wrap(pair + d, n_pair), pair).wait_send())
+        each(1, Y, lambda d: gather(k, wrap(y + d, Y), y).wait_send())
+
+        @pl.when(half == 0)
+        def _():
+            each(1, Y, lambda d: offer(k, wrap(y + d, Y), y).wait_send())
+            across(k).wait_send()
+
+    each(1, n_pair, lambda d: second(wrap(pair + d, n_pair), pair).wait_send())
+    each(1, n_pair, lambda d: g1(wrap(pair + d, n_pair), pair).wait_send())
+    each(1, Y, lambda d: g2(wrap(y + d, Y), y).wait_send())
+    s1().wait_send()
+    each(1, n_chip, lambda d: s2(wrap(chip + d, n_chip), chip).wait_send())
+    each(1, n_chip, lambda d: g3(wrap(chip + d, n_chip), pair).wait_send())
+    each(0, n_chip, lambda t: g4(2 * t + core).wait_send())
+
+
+def exchange(owner, blocks, one_t):
+    n_pair, s_count, _, packed, orbitals = blocks.shape
+    n_chip = n_pair // 2
+    width = n_pair * packed
+    rows = s_count * orbitals
+    chunk = 2 * width // n_pair
+    vmem = pl.BlockSpec(memory_space=pltpu.VMEM)
+    f32, bf16 = jnp.float32, jnp.bfloat16
+    sems = []
+    for shape in ((PIECES + 1, n_pair), (PIECES, Y), (PIECES,), (PIECES, Y), (n_pair,), (Y,), (n_chip,), (n_chip,),
+                  (1,), (n_chip,)):
+        sems += [pltpu.SemaphoreType.DMA(shape)] * 2
+    return pl.pallas_call(
+        exchange_kernel,
+        out_shape=(
+            jax.ShapeDtypeStruct((width, rows), bf16),
+            jax.ShapeDtypeStruct((2, width, rows), bf16),
+            jax.ShapeDtypeStruct((Y, width // Y // 8, 8, width), f32),
+            jax.ShapeDtypeStruct((chunk, width), bf16),
+        ),
+        in_specs=[pl.BlockSpec(memory_space=pltpu.SMEM), vmem, vmem],
+        out_specs=(vmem,) * 4,
+        scratch_shapes=[
+            pltpu.VMEM((2, n_pair, s_count, packed, orbitals), bf16),
+            pltpu.VMEM((width, width), bf16),
+            *[pltpu.VMEM((Y, width // Y, rows // PIECES), bf16)] * PIECES,
+            pltpu.VMEM((width // Y, width), f32),
+            pltpu.VMEM((n_pair, 8, BLOCK), f32),
+            pltpu.VMEM((n_chip, 2, chunk, width), bf16),
+            pltpu.VMEM((n_chip, chunk, width), bf16),
+            pltpu.VMEM((n_chip, chunk, width), bf16),
+            pltpu.VMEM((n_chip, chunk, width), bf16),
+            *sems,
+        ],
+        compiler_params=pltpu.CompilerParams(collective_id=0, has_side_effects=True, vmem_limit_bytes=32 << 20),
+        name="regroup_exchange",
+    )(owner, blocks, one_t)
+
+
 def share(value, axis):
     count = lax.axis_size(axis)
     return lax.all_to_all(jnp.broadcast_to(value[None], (count, *value.shape)), axis, 0, 0)
-
-
-def collect(value, axis):
-    count = lax.axis_size(axis)
-    return lax.all_to_all(value.reshape(count, value.shape[0] // count, *value.shape[1:]), axis, 0, 0)
-
-
-def build_block(moved, s_index, one_cols):
-    orbitals = moved.shape[0]
-    diagonal_mask = (s_index[:, None] == jnp.arange(orbitals, dtype=jnp.int32)[None, :]).astype(jnp.float32)
-    combined = diagonal_mask[:, None, None, :] * one_cols[None, :, :, None] - jnp.transpose(
-        moved, (3, 1, 2, 0)
-    ).astype(jnp.float32)
-    return combined.astype(jnp.bfloat16)
 
 
 def per_device(two_rdm, one_rdm, panel_block):
@@ -121,46 +361,36 @@
     groups = lax.axis_size("pair")
     s_count = orbitals // groups
     panel_width = RPAN * orbitals
-    pair_index = lax.axis_index("pair")
     col_index = lax.axis_index("col")
     first_orb = panel_block[0] * RPAN
-    s_index = pair_index * s_count + jnp.arange(s_count, dtype=jnp.int32)
-    one_cols = lax.dynamic_slice_in_dim(one_rdm, col_index * r_count, r_count, 1)
-    moved = lax.all_to_all(two_rdm, "pair", split_axis=3, concat_axis=0, tiled=True)
-    row_count = s_count * orbitals
-    col_count = r_count * orbitals
-    local_tile = build_block(moved, s_index, one_cols).reshape(row_count, col_count)
     owner_col = first_orb // r_count
     within = first_orb % r_count
-    panel_cols = lax.dynamic_slice_in_dim(local_tile, within * orbitals, panel_width, 1)
-    mine = lax.dynamic_index_in_dim(collect(panel_cols, "col"), owner_col, 0, keepdims=False)
-    panel = share(mine, "col").reshape(row_count, panel_width)
-    gram_part = lax.dot_general(panel, panel, (((0,), (0,)), ((), ())), preferred_element_type=jnp.float32)
-    gram = share(collect(gram_part, "pair").sum(0), "pair").reshape(panel_width, panel_width)
-    triangle, inverse = factor(gram, orbitals)
-    sums_part = lax.dot_general(
-        local_tile, panel, (((0,), (0,)), ((), ())), preferred_element_type=jnp.float32
-    ).astype(jnp.bfloat16)
-    sums_mine = collect(sums_part, "pair").astype(jnp.float32).sum(0).astype(jnp.bfloat16)
+    turned = lax.dynamic_slice_in_dim(jnp.concatenate([two_rdm, two_rdm], 2), within, r_count, 2)
+    blocks = jnp.transpose(turned, (3, 2, 0, 1)).reshape(groups, s_count, 2, RPAN * q_count, orbitals)
+    one_cols = lax.dynamic_slice_in_dim(one_rdm, col_index * r_count, r_count, 1)
+    one_t = lax.dynamic_slice_in_dim(jnp.concatenate([one_cols, one_cols], 1), within, r_count, 1).T
+    panel_t, tile_t, gram, sums_mine = exchange(owner_col[None], blocks, one_t)
+    triangle, inverse = factor(gram.reshape(panel_width, panel_width), orbitals)
+    col_count = r_count * orbitals
+    row_count = s_count * orbitals
     sums_t = share(sums_mine, "pair").reshape(col_count, panel_width)
+    tile_t = tile_t.reshape(col_count, row_count)
     inverse_hi = inverse.astype(jnp.bfloat16)
     inverse_lo = (inverse - inverse_hi.astype(jnp.float32)).astype(jnp.bfloat16)
 
-    def solve_right(value):
-        dims = (((1,), (1,)), ((), ()))
-        return (
-            lax.dot_general(value, inverse_hi, dims, preferred_element_type=jnp.float32)
-            + lax.dot_general(value, inverse_lo, dims, preferred_element_type=jnp.float32)
-        ).astype(jnp.bfloat16)
-
-    weights_t = solve_right(sums_t)
-    basis = solve_right(panel)
-    col_orb = col_index * r_count + jnp.arange(col_count, dtype=jnp.int32) // orbitals
-    trailing = col_orb >= first_orb + RPAN
-    product = lax.dot_general(basis, weights_t, (((1,), (1,)), ((), ())), preferred_element_type=jnp.float32)
-    refreshed = local_tile.astype(jnp.float32) - product
-    result = jnp.where(trailing[None, :], refreshed, local_tile.astype(jnp.float32)).astype(jnp.bfloat16)
-    return (result.reshape(s_count, orbitals, r_count, orbitals), triangle)
+    def times(a, b, dims):
+        return lax.dot_general(a, b, (dims, ((), ())), preferred_element_type=jnp.float32)
+
+    weights_t = (times(sums_t, inverse_hi, ((1,), (1,))) + times(sums_t, inverse_lo, ((1,), (1,)))).astype(jnp.bfloat16)
+    basis_t = (times(inverse_hi, panel_t, ((1,), (0,))) + times(inverse_lo, panel_t, ((1,), (0,)))).astype(jnp.bfloat16)
+    col_orb = col_index * r_count + (jnp.arange(r_count, dtype=jnp.int32) + within) % r_count
+    trailing = jnp.repeat(col_orb >= first_orb + RPAN, orbitals)
+    product = times(weights_t, basis_t, ((1,), (0,)))
+    kept = tile_t.astype(jnp.float32)
+    result = jnp.where(trailing[:, None], kept - product, kept).astype(jnp.bfloat16)
+    result = result.reshape(r_count, orbitals, s_count, orbitals)
+    result = lax.dynamic_slice_in_dim(jnp.concatenate([result, result], 0), r_count - within, r_count, 0)
+    return (jnp.transpose(result, (2, 3, 0, 1)), triangle)
 
 
 def solution(mesh):

time: 242 us -> 144 us (0.60)
  waiting for transfers between devices: 128 us -> 0.78 us
  Pallas kernels: 24.3 us -> 112 us
  starting transfers between devices: 42.9 us -> 6.93 us
  blocking collectives: 23.2 us -> 0 us
  other arithmetic: 1.42 us -> 4.08 us
    all_to_all x4 -> x0, waiting for transfers between devices: 98.7 us -> none  [the longest x3 71.7 us: collect(): lax.all_to_all(value.reshape(count, value.shape[0] // count, *value.shape...]
    pallas_call x0 -> x1, Pallas kernels: none -> 88.1 us  [exchange(): pl.pallas_call(exchange_kernel, out_shape=(jax.ShapeDtypeStruct((width, r...]
    all_to_all x4 -> x0, starting transfers between devices: 35.1 us -> none  [the longest x3 23.7 us: collect(): lax.all_to_all(value.reshape(count, value.shape[0] // count, *value.shape...]
    all_to_all x2 -> x1, waiting for transfers between devices: 28.9 us -> 0.78 us  [share(): lax.all_to_all(jnp.broadcast_to(value[None], (count, *value.shape)), axis...]
    all_to_all x1 -> x0, blocking collectives: 23.2 us -> none  [share(): lax.all_to_all(jnp.broadcast_to(value[None], (count, *value.shape)), axis...]
    transpose x0 -> x3, other arithmetic: none -> 4.06 us  [the longest x1 2.32 us: per_device(): jnp.transpose(turned, (3, 2, 0, 1))]
    dot_general x6 -> x4, matrix products: 11 us -> 9.94 us  [times(): lax.dot_general(a, b, (dims, ((), ())), preferred_element_type=jnp.float32)]
    all_to_all x2 -> x1, starting transfers between devices: 7.82 us -> 6.93 us  [share(): lax.all_to_all(jnp.broadcast_to(value[None], (count, *value.shape)), axis...]
  transfers between devices with their start and end apart: 6 -> 1, of which waited for: 6 -> 1; matrix products, arithmetic and copies ran while one was open for 2% -> 1% of each run, Pallas kernels for 10% -> 17%
where the time goes in v3:
time: 144 us; the launch traced here: 143 us
  Pallas kernels  112 us (78%)
  matrix products  9.94 us (7%)
  local copies, waits for them, and re-layouts  7.43 us (5%)
  starting transfers between devices  6.93 us (5%)
  other arithmetic  4.08 us (3%)
  between operations  1.46 us (1%)
    pallas_call x1, Pallas kernels, exchange(): pl.pallas_call(exchange_kernel, out_shape=(jax.ShapeDtypeStruct((width, r...  88.1 us
    pallas_call x1, Pallas kernels, factor(): pl.pallas_call(functools.partial(factor_kernel, scale), out_shape=(jax.Sh...  24.3 us
    dot_general x4, matrix products, times(): lax.dot_general(a, b, (dims, ((), ())), preferred_element_type=jnp.float32)  9.94 us
    all_to_all x1, starting transfers between devices, share(): lax.all_to_all(jnp.broadcast_to(value[None], (count, *value.shape)), axis...  6.93 us
  transfers between devices with their start and end apart: 1, of which 1 were waited for; matrix products, arithmetic and copies ran while one was open for 1% of the time, Pallas kernels for 17%

profile of v3, /device:TPU:1, one launch (start us, length us, event | category | flops | bytes accessed | tf_op | source)
XLA Modules:
  0.0 143.0 jit_solution(3530595978838665311)
XLA Ops:
  0.6 0.0 copy-start
  1.4 2.3 %fusion.5 = bf16[128,8,4,128]{0,1,3,2:T(8,128)(2,1)S(1)} fusion(s32[]{:T(128)S(6)} %select_n.34, bf16[4,128,8,128]{3,2,1,0:T(8,128)(2,1)} %param.3), kind=kLoop, calls=%fused_computation.12 | loop fusion | flops 2097152 | bytes 2097156 | tf_op jit(solution)/shard_map/transpose | solution.py:369
  3.7 1.8 %copy.5 = bf16[128,8,4,128]{3,2,1,0:T(4,128)(2,1)S(1)} copy(bf16[128,8,4,128]{0,1,3,2:T(8,128)(2,1)S(1)} %fusion.5) | data formatting | bytes 2097152 | tf_op jit(solution)/shard_map/transpose | solution.py:369
  5.5 0.0 copy-done
  5.5 0.1 constant_dynamic-slice_fusion
  5.6 0.1 copy.9
  5.7 88.1 %regroup_exchange.1 = (bf16[512,512]{1,0:T(8,128)(2,1)S(1)}, bf16[2,512,512]{2,1,0:T(8,128)(2,1)S(1)}, f32[8,8,8,512]{3,2,1,0:T(8,128)S(1)}, bf16[32,512]{1,0:T(8,128)(2,1)S(1)}) custom-call(s32[1]{0:T(128)} %bitcast.2.owner_ref, bf16[32,4,2,16,128]{4,3,2,1,0:T(8,128)(2,1)S(1)} %bitcast.20, f32[8,128]{1,0:T(8,128)S(1)} %fusion.7.one_ref), custom_call_target="tpu_custom_call" | custom-call | tf_op jit(solution)/shard_map/regroup_exchange/pallas_call | solution.py:327
  93.8 0.0 copy-start.1
  93.8 1.0 copy-done.1
  94.7 1.1 broadcast_in_dim.26
  95.8 6.9 %all-to-all-start = ((bf16[32,32,512]{2,1,0:T(8,128)(2,1)}), bf16[32,32,512]{2,1,0:T(8,128)(2,1)}, u32[]{:S(2)}, u32[]{:S(2)}) async-start(bf16[32,32,512]{2,1,0:T(8,128)(2,1)} %broadcast_in_dim.26), calls=%async_computation | async-start | bytes 2097152 | tf_op jit(solution)/shard_map/all_to_all | solution.py:356
  102.8 0.0 copy-start.2
  102.8 1.2 copy-done.2
  104.0 24.3 %panel_factor.1 = (f32[512,512]{1,0:T(8,128)}, f32[512,512]{1,0:T(8,128)S(1)}) custom-call(f32[512,512]{1,0:T(8,128)S(1)} %bitcast.22), custom_call_target="tpu_custom_call" | custom-call | flops 536870912 | bytes 3145728 | tf_op jit(solution)/shard_map/panel_factor/pallas_call | solution.py:91
  128.3 0.1 broadcast_bitcast_fusion
  128.4 1.5 %fusion.11 = f32[512,512]{1,0:T(8,128)} fusion(bf16[512,512]{1,0:T(8,128)(2,1)S(1)} %get-tuple-element.12, f32[512,512]{1,0:T(8,128)S(1)} %get-tuple-element.11), kind=kOutput, calls=%fused_computation.26 | convolution fusion | flops 268697600 | bytes 2621440 | tf_op jit(solution)/shard_map/dot_general | solution.py:382
  129.9 0.8 all-to-all-done
  130.7 2.0 %fusion.13 = f32[1024,512]{1,0:T(8,128)S(1)} fusion(bf16[1024,512]{1,0:T(8,128)(2,1)} %bitcast.7, f32[512,512]{1,0:T(8,128)S(1)} %get-tuple-element.11), kind=kOutput, calls=%fused_computation.28 | convolution fusion | flops 537133056 | bytes 4194304 | tf_op jit(solution)/shard_map/dot_general | solution.py:382
  132.6 2.9 %add_convert_fusion = bf16[1024,512]{1,0:T(8,128)(2,1)} fusion(f32[1024,512]{1,0:T(8,128)S(1)} %fusion.13, bf16[1024,512]{1,0:T(8,128)(2,1)} %bitcast.7, f32[512,512]{1,0:T(8,128)S(1)} %get-tuple-element.11), kind=kOutput, calls=%fused_computation.6 | convolution fusion | flops 538968064 | bytes 5242880 | tf_op jit(solution)/shard_map/dot_general | solution.py:382
  135.6 3.6 %fusion = bf16[1024,512]{1,0:T(8,128)(2,1)} fusion(bf16[1024,512]{1,0:T(8,128)(2,1)S(1)} %bitcast.21, bf16[1024,512]{1,0:T(8,128)(2,1)} %add_convert_fusion, f32[512,512]{1,0:T(8,128)} %fusion.11, bf16[512,512]{1,0:T(8,128)(2,1)S(1)} %get-tuple-element.12, pred[1024]{0:T(1024)(128)(4,1)S(1)} %broadcast_bitcast_fusion, f32[512,512]{1,0:T(8,128)S(1)} %get-tuple-element.11), kind=kOutput, calls=%fused_computation.1 | convolution fusion | flops 808976384 | bytes 5768192 | tf_op jit(solution)/shard_map/dot_general | solution.py:382
  139.2 1.3 reshape.26
  140.5 0.8 copy.7
  141.3 1.7 %fusion.3 = bf16[4,128,8,128]{3,2,1,0:T(8,128)(2,1)} fusion(s32[]{:T(128)S(6)} %select_n.37, bf16[8,128,4,128]{1,0,3,2:T(8,128)(2,1)S(1)} %copy.7), kind=kLoop, calls=%fused_computation.10 | loop fusion | flops 2097152 | bytes 2097156 | tf_op jit(solution)/shard_map/transpose | solution.py:393
  (2 shorter events, 0.0 us)
Async XLA Ops:
  0.6 4.9 %copy-start = (f32[128,128]{1,0:T(8,128)S(1)}, f32[128,128]{1,0:T(8,128)}, u32[]{:S(2)}) copy-start(f32[128,128]{1,0:T(8,128)} %param.4) | copy-start | bytes 196612
  93.8 1.0 copy-start.1
  95.8 34.8 %all-to-all-start = ((bf16[32,32,512]{2,1,0:T(8,128)(2,1)}), bf16[32,32,512]{2,1,0:T(8,128)(2,1)}, u32[]{:S(2)}, u32[]{:S(2)}) async-start(bf16[32,32,512]{2,1,0:T(8,128)(2,1)} %broadcast_in_dim.26), calls=%async_computation | async-start | bytes 2097152 | tf_op jit(solution)/shard_map/all_to_all | solution.py:356
  102.8 1.2 copy-start.2

commit v4 on v3

--- a/solution.py
+++ b/solution.py
@@ -51,7 +51,7 @@
             work[s0:BLOCK, BLOCK:] = work[s0:BLOCK, BLOCK:] - delta_b
 
 
-def factor_kernel(scale, gram_ref, tri_ref, inv_ref, aug, work):
+def finish_kernel(scale, flag_ref, gram_ref, sums_ref, panel_ref, tile_ref, tri_ref, out_ref, aug, work, outer):
     n = gram_ref.shape[0]
     row = lax.broadcasted_iota(jnp.int32, (n, n), 0)
     col = lax.broadcasted_iota(jnp.int32, (n, n), 1)
@@ -82,22 +82,51 @@
 
     lax.fori_loop(0, n // BLOCK, step, 0)
     tri_ref[...] = jnp.where(row <= col, aug[:, :n], 0.0) / scale
-    inv_ref[...] = jnp.where(row >= col, aug[:, n:], 0.0)
-
-
-def factor(gram, scale):
+    inverse = jnp.where(row >= col, aug[:, n:], 0.0)
+    high = inverse.astype(jnp.bfloat16)
+    low = (inverse - high.astype(jnp.float32)).astype(jnp.bfloat16)
+
+    def times(a, b, dims):
+        return lax.dot_general(a, b, (dims, ((), ())), preferred_element_type=jnp.float32)
+
+    basis_t = (times(high, panel_ref[...], ((1,), (0,))) + times(low, panel_ref[...], ((1,), (0,)))).astype(jnp.bfloat16)
+    s_count, orbitals, r_count, _ = out_ref.shape
+    per_half = r_count // 2
+    for h in range(2):
+        source = flag_ref[2 + h]
+        sums = sums_ref[source]
+        weights_t = (times(sums, high, ((1,), (1,))) + times(sums, low, ((1,), (1,)))).astype(jnp.bfloat16)
+        product = times(weights_t, basis_t, ((1,), (0,)))
+        outer[h] = tile_ref[source].astype(jnp.float32) - jnp.where(flag_ref[h] > 0, product, 0.0)
+    for s in range(s_count):
+        parts = [
+            outer[h, r * BLOCK:(r + 1) * BLOCK, s * orbitals:(s + 1) * orbitals].T
+            for h in range(2) for r in range(per_half)
+        ]
+        out_ref[s] = jnp.stack(parts, axis=1).astype(jnp.bfloat16)
+
+
+def finish(flags, gram, sums, panel_t, tile_t, s_count, scale):
     n = gram.shape[0]
+    rows = panel_t.shape[1]
     whole = pl.BlockSpec(memory_space=pltpu.VMEM)
     return pl.pallas_call(
-        functools.partial(factor_kernel, scale),
-        out_shape=(jax.ShapeDtypeStruct((n, n), jnp.float32),) * 2,
-        in_specs=[whole],
+        functools.partial(finish_kernel, scale),
+        out_shape=(
+            jax.ShapeDtypeStruct((n, n), jnp.float32),
+            jax.ShapeDtypeStruct((s_count, rows // s_count, 2 * n // BLOCK, BLOCK), jnp.bfloat16),
+        ),
+        in_specs=[pl.BlockSpec(memory_space=pltpu.SMEM)] + [whole] * 4,
         out_specs=(whole,) * 2,
-        scratch_shapes=[pltpu.VMEM((n, 2 * n), jnp.float32), pltpu.VMEM((BLOCK, 2 * BLOCK), jnp.float32)],
-        compiler_params=pltpu.CompilerParams(vmem_limit_bytes=16 << 20),
-        cost_estimate=pl.CostEstimate(flops=4 * n**3, bytes_accessed=12 * n * n, transcendentals=n),
-        name="panel_factor",
-    )(gram)
+        scratch_shapes=[
+            pltpu.VMEM((n, 2 * n), jnp.float32),
+            pltpu.VMEM((BLOCK, 2 * BLOCK), jnp.float32),
+            pltpu.VMEM((2, n, rows), jnp.float32),
+        ],
+        compiler_params=pltpu.CompilerParams(vmem_limit_bytes=32 << 20),
+        cost_estimate=pl.CostEstimate(flops=16 * n**3, bytes_accessed=24 * n * n, transcendentals=n),
+        name="factor_apply",
+    )(flags, gram, sums, panel_t, tile_t)
 
 
 def wrap(value, count):
@@ -108,10 +137,11 @@
     lax.fori_loop(start, stop, lambda k, c: (body(k), c)[1], 0)
 
 
-def exchange_kernel(owner_ref, x_ref, one_ref, panel_ref, gt_ref, gram_ref, mine_ref,
+def exchange_kernel(owner_ref, x_ref, one_ref, panel_ref, gt_ref, gram_ref, sums_ref,
                     land, order, picks_a, picks_b, gpart, gin, spart, score, shalf, sin,
                     a_send, a_recv, p_send, p_recv, q_send, q_recv, c_send, c_recv, g1_send, g1_recv, g2_send, g2_recv,
-                    g3_send, g3_recv, g4_send, g4_recv, s1_send, s1_recv, s2_send, s2_recv):
+                    g3_send, g3_recv, h2_send, h2_recv, h3_send, h3_recv, g4_send, g4_recv,
+                    s1_send, s1_recv, s2_send, s2_recv, s3_send, s3_recv, s4_send, s4_recv):
     pair = lax.axis_index("pair")
     colm = lax.axis_index("col")
     n_pair = lax.axis_size("pair")
@@ -145,10 +175,17 @@
 
     def first(k, peer, slot):
         ss = pl.ds(k * s_piece, s_piece)
-        return on_pair(x_ref.at[peer, ss, 0], land.at[0, slot, ss], a_send.at[k, peer], a_recv.at[k, slot], peer)
+        return on_pair(x_ref.at[peer, ss, 0], land.at[0, slot, ss], a_send.at[k], a_recv.at[k], peer)
 
     def second(peer, slot):
-        return on_pair(x_ref.at[peer, :, 1], land.at[1, slot], a_send.at[PIECES, peer], a_recv.at[PIECES, slot], peer)
+        return on_pair(x_ref.at[peer, :, 1], land.at[1, slot], a_send.at[PIECES], a_recv.at[PIECES], peer)
+
+    def all_first(k):
+        ss = pl.ds(k * s_piece, s_piece)
+        return on_pair(x_ref.at[1:, ss, 0], land.at[0, 1:, ss], a_send.at[k], a_recv.at[k], other_core)
+
+    def all_second():
+        return on_pair(x_ref.at[1:, :, 1], land.at[1, 1:], a_send.at[PIECES], a_recv.at[PIECES], other_core)
 
     for k in range(PIECES):
         each(1, n_pair, lambda d: first(k, wrap(pair + d, n_pair), pair).start())
@@ -176,7 +213,7 @@
 
     def offer(piece, k, slot):
         rows, lanes = block(k, piece)
-        return on_col(gt_ref.at[0, rows, lanes], picks[piece].at[slot], p_send.at[piece, k], p_recv.at[piece, slot], k)
+        return on_col(gt_ref.at[0, rows, lanes], picks[piece].at[slot], p_send.at[piece], p_recv.at[piece], k)
 
     def across(piece):
         where = panel_ref.at[block(y, piece)]
@@ -184,10 +221,19 @@
 
     def gather(piece, k, row):
         where = panel_ref.at[block(row, piece)]
-        return on_col(where, where, c_send.at[piece, k], c_recv.at[piece, row], half * Y + k)
+        return on_col(where, where, c_send.at[piece], c_recv.at[piece], half * Y + k)
+
+    def all_offers(piece):
+        lanes = pl.ds(piece * span, span)
+        return on_col(gt_ref.at[0, :(Y - 1) * part, lanes], picks[piece].at[1:], p_send.at[piece], p_recv.at[piece],
+                      (1 - half) * Y + y)
+
+    def all_gathers(piece):
+        where = panel_ref.at[:(Y - 1) * part, pl.ds(piece * span, span)]
+        return on_col(where, where, c_send.at[piece], c_recv.at[piece], (1 - half) * Y + y)
 
     for piece in range(PIECES):
-        each(1, n_pair, lambda d: first(piece, wrap(pair + d, n_pair), wrap(pair + d, n_pair)).wait_recv())
+        all_first(piece).wait_recv()
         for s in range(piece * s_piece, (piece + 1) * s_piece):
             build(0, s)
 
@@ -202,7 +248,7 @@
     for piece in range(PIECES):
         @pl.when(half == 0)
         def _():
-            each(1, Y, lambda d: offer(piece, wrap(y + d, Y), wrap(y + d, Y)).wait_recv())
+            all_offers(piece).wait_recv()
             rows, lanes = block(y, piece)
             panel_ref[rows, lanes] = picks[piece][owner_ref[0]]
             across(piece).start()
@@ -213,13 +259,13 @@
 
         each(1, Y, lambda d: gather(piece, wrap(y + d, Y), y).start())
 
-    each(1, n_pair, lambda d: second(wrap(pair + d, n_pair), wrap(pair + d, n_pair)).wait_recv())
+    all_second().wait_recv()
     for s in range(s_count):
         build(1, s)
     for piece in range(PIECES):
-        each(1, Y, lambda d: gather(piece, wrap(y + d, Y), wrap(y + d, Y)).wait_recv())
-
-    chunk = mine_ref.shape[0]
+        all_gathers(piece).wait_recv()
+
+    chunk = sums_ref.shape[2]
     rows_at_once = 2 * BLOCK
     count = rows_at_once // (2 * chunk)
     for h in range(2):
@@ -242,7 +288,7 @@
 
     def g1(i, slot):
         src = gpart.at[pl.ds(pl.multiple_of((i // wide) * 8, 8), 8), column(lax.rem(i, wide))]
-        return on_pair(src, gin.at[slot], g1_send.at[i], g1_recv.at[slot], i)
+        return on_pair(src, gin.at[slot], g1_send.at[0], g1_recv.at[0], i)
 
     each(1, n_pair, lambda d: g1(wrap(pair + d, n_pair), pair).start())
     my_r, my_c = pair // wide, lax.rem(pair, wide)
@@ -256,60 +302,138 @@
     each(0, n_chip, add_cores)
 
     def s2(t, slot):
-        return on_pair(shalf.at[t], sin.at[slot], s2_send.at[t], s2_recv.at[slot], 2 * t + core)
+        return on_pair(shalf.at[t], sin.at[slot], s2_send.at[0], s2_recv.at[0], 2 * t + core)
 
     each(1, n_chip, lambda d: s2(wrap(chip + d, n_chip), chip).start())
     sin[chip] = shalf[chip]
 
-    each(1, n_pair, lambda d: g1(wrap(pair + d, n_pair), wrap(pair + d, n_pair)).wait_recv())
+    def all_g1():
+        return on_pair(gin.at[1:], gin.at[1:], g1_send.at[0], g1_recv.at[0], other_core)
+
+    def all_s2():
+        return on_pair(shalf.at[1:], sin.at[1:], s2_send.at[0], s2_recv.at[0], other_core)
+
+    all_g1().wait_recv()
     gram_ref[y, my_r, :, column(my_c)] = jnp.sum(gin[...], axis=0)
 
-    def g2(k, row):
-        where = gram_ref.at[row, my_r, :, column(my_c)]
-        return on_col(where, where, g2_send.at[k], g2_recv.at[row], half * Y + k)
-
-    each(1, Y, lambda d: g2(wrap(y + d, Y), y).start())
-    each(1, Y, lambda d: g2(wrap(y + d, Y), wrap(y + d, Y)).wait_recv())
-
-    def held(source):
-        return gram_ref.at[:, source // wide, :, column(lax.rem(source, wide))]
-
-    def g3(t, source):
-        return on_pair(held(source), held(source), g3_send.at[t], g3_recv.at[source // 2], 2 * t + core)
-
-    def g4(source):
-        return on_pair(held(source), held(source), g4_send.at[source // 2], g4_recv.at[source // 2], other_core)
-
-    each(1, n_chip, lambda d: g3(wrap(chip + d, n_chip), pair).start())
-    g4(pair).start()
-
-    each(1, n_chip, lambda d: s2(wrap(chip + d, n_chip), wrap(chip + d, n_chip)).wait_recv())
-    mine_ref[...] = jnp.sum(sin[...].astype(jnp.float32), axis=0).astype(jnp.bfloat16)
-
-    def forward(d):
-        source = 2 * wrap(chip + n_chip - d, n_chip) + core
-        g3(source // 2, source).wait_recv()
-        g4(source).start()
-
-    each(1, n_chip, forward)
-    each(0, n_chip, lambda t: g4(2 * t + 1 - core).wait_recv())
-
-    for k in range(PIECES):
-        each(1, n_pair, lambda d: first(k, wrap(pair + d, n_pair), pair).wait_send())
-        each(1, Y, lambda d: gather(k, wrap(y + d, Y), y).wait_send())
+    early = lax.rem(chip, 2) == 0
+    top, bottom = column(core), column(2 + core)
+    mine = gram_ref.at[y, my_r, :, column(my_c)]
+    tall = gram_ref.at[:, my_r, :, top]
+    flat = gram_ref.at[y, :, :, bottom]
+
+    def g2(k):
+        return on_col(mine, mine, g2_send.at[0], g2_recv.at[0], half * Y + k)
+
+    def all_g2():
+        where = gram_ref.at[1:, my_r, :, top]
+        return on_col(where, where, g2_send.at[0], g2_recv.at[0], (1 - half) * Y + y)
+
+    def g3(t):
+        return on_pair(tall, tall, g3_send.at[t], g3_recv.at[0], 2 * t + core)
+
+    def h2(t):
+        return on_pair(mine, mine, h2_send.at[t], h2_recv.at[0], 2 * t + core)
+
+    def h3(k):
+        return on_col(flat, flat, h3_send.at[0], h3_recv.at[0], half * Y + k)
+
+    def all_h3():
+        where = gram_ref.at[1:, :, :, bottom]
+        return on_col(where, where, h3_send.at[0], h3_recv.at[0], (1 - half) * Y + y)
+
+    def some_g3(count):
+        where = gram_ref.at[:, :count, :, top]
+        return on_pair(where, where, g3_send.at[0], g3_recv.at[0], other_core)
+
+    def some_h2(count):
+        where = gram_ref.at[y, :count, :, bottom]
+        return on_pair(where, where, h2_send.at[0], h2_recv.at[0], other_core)
+
+    r_tiles = n_chip // 2
+
+    @pl.when(early)
+    def _():
+        each(1, Y, lambda d: g2(wrap(y + d, Y)).start())
+        some_h2(r_tiles).wait_recv()
+        each(1, Y, lambda d: h3(wrap(y + d, Y)).start())
+        all_g2().wait_recv()
+        each(1, n_chip, lambda d: g3(wrap(chip + d, n_chip)).start())
+
+    @pl.when(jnp.logical_not(early))
+    def _():
+        each(1, n_chip, lambda d: h2(wrap(chip + d, n_chip)).start())
+        some_h2(r_tiles - 1).wait_recv()
+        each(1, Y, lambda d: h3(wrap(y + d, Y)).start())
+
+    def s3(t):
+        return on_pair(sums_ref.at[chip, core], sums_ref.at[chip, core], s3_send.at[0], s3_recv.at[0], 2 * t + core)
+
+    def all_s3():
+        where = sums_ref.at[1:, core]
+        return on_pair(where, where, s3_send.at[0], s3_recv.at[0], other_core)
+
+    def s4():
+        return on_pair(sums_ref.at[:, core], sums_ref.at[:, core], s4_send.at[0], s4_recv.at[0], other_core)
+
+    def arrived_s4():
+        where = sums_ref.at[:, 1 - core]
+        return on_pair(where, where, s4_send.at[0], s4_recv.at[0], other_core)
+
+    def g4(k, lanes):
+        where = gram_ref.at[:, :, :, lanes]
+        return on_pair(where, where, g4_send.at[k], g4_recv.at[k], other_core)
+
+    all_s2().wait_recv()
+    sums_ref[chip, core] = jnp.sum(sin[...].astype(jnp.float32), axis=0).astype(jnp.bfloat16)
+    each(1, n_chip, lambda d: s3(wrap(chip + d, n_chip)).start())
+
+    all_h3().wait_recv()
+    g4(1, bottom).start()
+
+    @pl.when(early)
+    def _():
+        some_g3(r_tiles - 1).wait_recv()
+
+    @pl.when(jnp.logical_not(early))
+    def _():
+        some_g3(r_tiles).wait_recv()
+
+    g4(0, top).start()
+    all_s3().wait_recv()
+    s4().start()
+    g4(1, column(3 - core)).wait_recv()
+    g4(0, column(1 - core)).wait_recv()
+    arrived_s4().wait_recv()
+
+    for piece in range(PIECES):
+        all_first(piece).wait_send()
+        all_gathers(piece).wait_send()
 
         @pl.when(half == 0)
         def _():
-            each(1, Y, lambda d: offer(k, wrap(y + d, Y), y).wait_send())
-            across(k).wait_send()
-
-    each(1, n_pair, lambda d: second(wrap(pair + d, n_pair), pair).wait_send())
-    each(1, n_pair, lambda d: g1(wrap(pair + d, n_pair), pair).wait_send())
-    each(1, Y, lambda d: g2(wrap(y + d, Y), y).wait_send())
+            all_offers(piece).wait_send()
+            across(piece).wait_send()
+
+    all_second().wait_send()
     s1().wait_send()
-    each(1, n_chip, lambda d: s2(wrap(chip + d, n_chip), chip).wait_send())
-    each(1, n_chip, lambda d: g3(wrap(chip + d, n_chip), pair).wait_send())
-    each(0, n_chip, lambda t: g4(2 * t + core).wait_send())
+    all_g1().wait_send()
+    all_s2().wait_send()
+
+    @pl.when(early)
+    def _():
+        all_g2().wait_send()
+        each(1, n_chip, lambda d: g3(wrap(chip + d, n_chip)).wait_send())
+
+    @pl.when(jnp.logical_not(early))
+    def _():
+        each(1, n_chip, lambda d: h2(wrap(chip + d, n_chip)).wait_send())
+
+    g4(0, top).wait_send()
+    g4(1, bottom).wait_send()
+    all_h3().wait_send()
+    all_s3().wait_send()
+    s4().wait_send()
 
 
 def exchange(owner, blocks, one_t):
@@ -321,16 +445,16 @@
     vmem = pl.BlockSpec(memory_space=pltpu.VMEM)
     f32, bf16 = jnp.float32, jnp.bfloat16
     sems = []
-    for shape in ((PIECES + 1, n_pair), (PIECES, Y), (PIECES,), (PIECES, Y), (n_pair,), (Y,), (n_chip,), (n_chip,),
-                  (1,), (n_chip,)):
-        sems += [pltpu.SemaphoreType.DMA(shape)] * 2
+    for send, recv in ((PIECES + 1,) * 2, (PIECES,) * 2, (PIECES,) * 2, (PIECES,) * 2, (1, 1), (1, 1), (n_chip, 1),
+                       (n_chip, 1), (1, 1), (2, 2), (1, 1), (1, 1), (1, 1), (1, 1)):
+        sems += [pltpu.SemaphoreType.DMA((send,)), pltpu.SemaphoreType.DMA((recv,))]
     return pl.pallas_call(
         exchange_kernel,
         out_shape=(
             jax.ShapeDtypeStruct((width, rows), bf16),
             jax.ShapeDtypeStruct((2, width, rows), bf16),
             jax.ShapeDtypeStruct((Y, width // Y // 8, 8, width), f32),
-            jax.ShapeDtypeStruct((chunk, width), bf16),
+            jax.ShapeDtypeStruct((n_chip, 2, chunk, width), bf16),
         ),
         in_specs=[pl.BlockSpec(memory_space=pltpu.SMEM), vmem, vmem],
         out_specs=(vmem,) * 4,
@@ -351,11 +475,6 @@
     )(owner, blocks, one_t)
 
 
-def share(value, axis):
-    count = lax.axis_size(axis)
-    return lax.all_to_all(jnp.broadcast_to(value[None], (count, *value.shape)), axis, 0, 0)
-
-
 def per_device(two_rdm, one_rdm, panel_block):
     q_count, orbitals, r_count, _ = two_rdm.shape
     groups = lax.axis_size("pair")
@@ -369,28 +488,14 @@
     blocks = jnp.transpose(turned, (3, 2, 0, 1)).reshape(groups, s_count, 2, RPAN * q_count, orbitals)
     one_cols = lax.dynamic_slice_in_dim(one_rdm, col_index * r_count, r_count, 1)
     one_t = lax.dynamic_slice_in_dim(jnp.concatenate([one_cols, one_cols], 1), within, r_count, 1).T
-    panel_t, tile_t, gram, sums_mine = exchange(owner_col[None], blocks, one_t)
-    triangle, inverse = factor(gram.reshape(panel_width, panel_width), orbitals)
-    col_count = r_count * orbitals
-    row_count = s_count * orbitals
-    sums_t = share(sums_mine, "pair").reshape(col_count, panel_width)
-    tile_t = tile_t.reshape(col_count, row_count)
-    inverse_hi = inverse.astype(jnp.bfloat16)
-    inverse_lo = (inverse - inverse_hi.astype(jnp.float32)).astype(jnp.bfloat16)
-
-    def times(a, b, dims):
-        return lax.dot_general(a, b, (dims, ((), ())), preferred_element_type=jnp.float32)
-
-    weights_t = (times(sums_t, inverse_hi, ((1,), (1,))) + times(sums_t, inverse_lo, ((1,), (1,)))).astype(jnp.bfloat16)
-    basis_t = (times(inverse_hi, panel_t, ((1,), (0,))) + times(inverse_lo, panel_t, ((1,), (0,)))).astype(jnp.bfloat16)
-    col_orb = col_index * r_count + (jnp.arange(r_count, dtype=jnp.int32) + within) % r_count
-    trailing = jnp.repeat(col_orb >= first_orb + RPAN, orbitals)
-    product = times(weights_t, basis_t, ((1,), (0,)))
-    kept = tile_t.astype(jnp.float32)
-    result = jnp.where(trailing[:, None], kept - product, kept).astype(jnp.bfloat16)
-    result = result.reshape(r_count, orbitals, s_count, orbitals)
-    result = lax.dynamic_slice_in_dim(jnp.concatenate([result, result], 0), r_count - within, r_count, 0)
-    return (jnp.transpose(result, (2, 3, 0, 1)), triangle)
+    panel_t, tile_t, gram, sums_t = exchange(owner_col[None], blocks, one_t)
+    starts = col_index * r_count + jnp.arange(2, dtype=jnp.int32) * RPAN
+    place = (jnp.arange(2, dtype=jnp.int32) + within // RPAN) % 2
+    flags = jnp.concatenate([(starts >= first_orb + RPAN).astype(jnp.int32), place])
+    sums_t = sums_t.reshape(2, panel_width, panel_width)
+    triangle, updated = finish(
+        flags, gram.reshape(panel_width, panel_width), sums_t, panel_t, tile_t, s_count, orbitals)
+    return updated, triangle
 
 
 def solution(mesh):

time: 144 us -> 129 us (0.90)
  Pallas kernels: 112 us -> 122 us
  matrix products: 9.94 us -> 0 us
  starting transfers between devices: 6.93 us -> 0 us
  local copies, waits for them, and re-layouts: 7.43 us -> 1.94 us
  other arithmetic: 4.08 us -> 2.51 us
    dot_general x4 -> x0, matrix products: 9.94 us -> none  [times(): lax.dot_general(a, b, (dims, ((), ())), preferred_element_type=jnp.float32)]
    all_to_all x1 -> x0, starting transfers between devices: 6.93 us -> none  [share(): lax.all_to_all(jnp.broadcast_to(value[None], (count, *value.shape)), axis...]
    pallas_call x1, Pallas kernels: 88.1 us -> 93.6 us  [exchange(): pl.pallas_call(exchange_kernel, out_shape=(jax.ShapeDtypeStruct((width, r...]
    pallas_call x1, Pallas kernels: 24.3 us -> 28.9 us  [finish(): pl.pallas_call(functools.partial(finish_kernel, scale), out_shape=(jax.Sh...]
    unnamed x7 -> x3, local copies, waits for them, and re-layouts: 2.25 us -> 0.06 us
    reshape x2 -> x0, local copies, waits for them, and re-layouts: 2.14 us -> none  [per_device(): result = result.reshape(r_count, orbitals, s_count, orbitals)]
    transpose x1 -> x0, other arithmetic: 1.73 us -> none  [per_device(): return (jnp.transpose(result, (2, 3, 0, 1)), triangle)]
  transfers between devices with their start and end apart: 1 -> 0, of which waited for: 1 -> 0; matrix products, arithmetic and copies ran while one was open for 1% -> 0% of each run, Pallas kernels for 17% -> 0%
where the time goes in v4:
time: 129 us; the launch traced here: 128 us
  Pallas kernels  122 us (95%)
  other arithmetic  2.51 us (2%)
  local copies, waits for them, and re-layouts  1.94 us (2%)
  between operations  1.43 us (1%)
    pallas_call x1, Pallas kernels, exchange(): pl.pallas_call(exchange_kernel, out_shape=(jax.ShapeDtypeStruct((width, r...  93.6 us
    pallas_call x1, Pallas kernels, finish(): pl.pallas_call(functools.partial(finish_kernel, scale), out_shape=(jax.Sh...  28.9 us

profile of v4, /device:TPU:1, one launch (start us, length us, event | category | flops | bytes accessed | tf_op | source)
XLA Modules:
  0.0 128.3 jit_solution(14960519782931750907)
XLA Ops:
  0.6 0.0 copy-start
  1.4 0.1 pad_add_fusion.flag_ref
  1.5 0.0 copy-done
  1.5 0.1 constant_dynamic-slice_fusion
  1.6 0.1 copy.7
  1.7 2.4 %fusion.1 = bf16[128,8,4,128]{0,1,3,2:T(8,128)(2,1)S(1)} fusion(s32[]{:T(128)S(6)} %select_n.31, bf16[4,128,8,128]{3,2,1,0:T(8,128)(2,1)} %param.3), kind=kLoop, calls=%fused_computation.3 | loop fusion | flops 2097152 | bytes 2097156 | tf_op jit(solution)/shard_map/transpose | solution.py:488
  4.1 1.8 %copy.5 = bf16[128,8,4,128]{3,2,1,0:T(4,128)(2,1)S(1)} copy(bf16[128,8,4,128]{0,1,3,2:T(8,128)(2,1)S(1)} %fusion.1) | data formatting | bytes 2097152 | tf_op jit(solution)/shard_map/transpose | solution.py:488
  5.9 93.6 %regroup_exchange.1 = (bf16[512,512]{1,0:T(8,128)(2,1)S(1)}, bf16[2,512,512]{2,1,0:T(8,128)(2,1)S(1)}, f32[8,8,8,512]{3,2,1,0:T(8,128)S(1)}, bf16[16,2,32,512]{3,2,1,0:T(8,128)(2,1)S(1)}) custom-call(s32[1]{0:T(128)} %bitcast.1.owner_ref, bf16[32,4,2,16,128]{4,3,2,1,0:T(8,128)(2,1)S(1)} %bitcast.9, f32[8,128]{1,0:T(8,128)S(1)} %fusion.3.one_ref), custom_call_target="tpu_custom_call" | custom-call | tf_op jit(solution)/shard_map/regroup_exchange/pallas_call | solution.py:451
  99.5 28.9 %factor_apply.1 = (f32[512,512]{1,0:T(8,128)}, bf16[4,128,8,128]{3,2,1,0:T(8,128)(2,1)}) custom-call(s32[4]{0:T(128)S(1)} %pad_add_fusion.flag_ref, f32[512,512]{1,0:T(8,128)S(1)} %bitcast.10, bf16[2,512,512]{2,1,0:T(8,128)(2,1)S(1)} %bitcast.11, bf16[512,512]{1,0:T(8,128)(2,1)S(1)} %get-tuple-element.10.panel_ref, ...), custom_call_target="tpu_custom_call" | custom-call | flops 2147483648 | bytes 6291456 | tf_op jit(solution)/shard_map/factor_apply/pallas_call | solution.py:113
  (3 shorter events, 0.0 us)
Async XLA Ops:
  0.6 0.9 copy-start

commit v5 on v4

--- a/solution.py
+++ b/solution.py
@@ -9,7 +9,7 @@
 
 RPAN = 4
 BLOCK = 128
-STRIP = 4
+STRIP = 8
 EXACT = lax.Precision.HIGHEST
 MESH = pl.DeviceIdType.MESH
 PIECES = 2
@@ -18,85 +18,93 @@
 
 def factor_block(work):
     for k in range(0, BLOCK, STRIP):
-        r0 = (k // 8) * 8
-        left = work[r0:BLOCK, 0:BLOCK]
-        cols = [jnp.broadcast_to(left[:, k + j : k + j + 1], (BLOCK - r0, BLOCK)) for j in range(STRIP)]
-        rows = [work[k + j : k + j + 1, :] for j in range(STRIP)]
-        entry = {(i, j): cols[j][k + i - r0 : k + i - r0 + 1, :] for j in range(STRIP) for i in range(j, STRIP)}
+        tiles = (BLOCK - k) // STRIP
+        left = work[k:BLOCK, 0:BLOCK]
+        cols = [
+            jnp.broadcast_to(left[:, k + j : k + j + 1], (BLOCK - k, BLOCK)).reshape(tiles, STRIP, BLOCK)
+            for j in range(STRIP)
+        ]
+        rows_a = [jnp.broadcast_to(work[k + j : k + j + 1, :BLOCK], (STRIP, BLOCK)) for j in range(STRIP)]
+        rows_b = [jnp.broadcast_to(work[k + j : k + j + 1, BLOCK:], (STRIP, BLOCK)) for j in range(STRIP)]
+        entry = {
+            (i, j): jnp.broadcast_to(cols[j][0, i : i + 1, :], (STRIP, BLOCK)) for j in range(STRIP) for i in range(j, STRIP)
+        }
         for j in range(STRIP):
             inv = lax.rsqrt(entry[j, j])
-            rows[j] = rows[j] * jnp.concatenate([inv, inv], axis=1)
-            cols[j] = cols[j] * inv
+            rows_a[j] = rows_a[j] * inv
+            rows_b[j] = rows_b[j] * inv
+            cols[j] = cols[j] * inv[None]
             low = {i: entry[i, j] * inv for i in range(j + 1, STRIP)}
             for i in range(j + 1, STRIP):
                 for m in range(j + 1, i + 1):
                     entry[i, m] = entry[i, m] - low[i] * low[m]
-                rows[i] = rows[i] - jnp.concatenate([low[i], low[i]], axis=1) * rows[j]
-                cols[i] = cols[i] - low[i] * cols[j]
+                rows_a[i] = rows_a[i] - low[i] * rows_a[j]
+                rows_b[i] = rows_b[i] - low[i] * rows_b[j]
+                cols[i] = cols[i] - low[i][None] * cols[j]
         for j in range(STRIP):
-            work[k + j : k + j + 1, :] = rows[j]
-        t0 = k + STRIP
-        if t0 < BLOCK:
-            s0 = (t0 // 8) * 8
+            work[k + j : k + j + 1, :BLOCK] = rows_a[j][0:1]
+            work[k + j : k + j + 1, BLOCK:] = rows_b[j][0:1]
+        if tiles > 1:
             delta_a, delta_b = 0.0, 0.0
             for j in range(STRIP):
-                c = cols[j][s0 - r0 :, :]
-                delta_a = delta_a + c * rows[j][:, :BLOCK]
-                delta_b = delta_b + c * rows[j][:, BLOCK:]
-            if s0 < t0:
-                below = lax.broadcasted_iota(jnp.int32, (BLOCK - s0, BLOCK), 0) + s0 >= t0
-                delta_a = jnp.where(below, delta_a, 0.0)
-                delta_b = jnp.where(below, delta_b, 0.0)
-            work[s0:BLOCK, :BLOCK] = work[s0:BLOCK, :BLOCK] - delta_a
-            work[s0:BLOCK, BLOCK:] = work[s0:BLOCK, BLOCK:] - delta_b
-
-
-def finish_kernel(scale, flag_ref, gram_ref, sums_ref, panel_ref, tile_ref, tri_ref, out_ref, aug, work, outer):
+                delta_a = delta_a + cols[j][1:] * rows_a[j][None]
+                delta_b = delta_b + cols[j][1:] * rows_b[j][None]
+            below = BLOCK - k - STRIP
+            work[k + STRIP : BLOCK, :BLOCK] = work[k + STRIP : BLOCK, :BLOCK] - delta_a.reshape(below, BLOCK)
+            work[k + STRIP : BLOCK, BLOCK:] = work[k + STRIP : BLOCK, BLOCK:] - delta_b.reshape(below, BLOCK)
+
+
+def finish_kernel(scale, flag_ref, gram_ref, sums_ref, panel_ref, tile_ref, tri_ref, out_ref,
+                  left, right, work, basis, weights, outer):
     n = gram_ref.shape[0]
-    row = lax.broadcasted_iota(jnp.int32, (n, n), 0)
-    col = lax.broadcasted_iota(jnp.int32, (n, n), 1)
-    aug[:, :n] = gram_ref[...]
-    aug[:, n:] = (row == col).astype(jnp.float32)
     eye = (
         lax.broadcasted_iota(jnp.int32, (BLOCK, BLOCK), 0) == lax.broadcasted_iota(jnp.int32, (BLOCK, BLOCK), 1)
     ).astype(jnp.float32)
-
-    def step(b, carry):
-        o = pl.multiple_of(b * BLOCK, BLOCK)
-        work[:, :BLOCK] = aug[pl.ds(o, BLOCK), pl.ds(o, BLOCK)]
-        work[:, BLOCK:] = eye
-        factor_block(work)
-        aug[pl.ds(o, BLOCK), :] = jnp.dot(
-            work[:, BLOCK:], aug[pl.ds(o, BLOCK), :], precision=EXACT, preferred_element_type=jnp.float32
-        )
-
-        def trail(m, carry):
-            q = pl.multiple_of(m * BLOCK, BLOCK)
-            u = aug[pl.ds(o, BLOCK), pl.ds(q, BLOCK)]
-            aug[pl.ds(q, BLOCK), :] -= lax.dot_general(
-                u, aug[pl.ds(o, BLOCK), :], (((0,), (0,)), ((), ())), precision=EXACT, preferred_element_type=jnp.float32
-            )
-            return carry
-
-        return lax.fori_loop(b + 1, n // BLOCK, trail, carry)
-
-    lax.fori_loop(0, n // BLOCK, step, 0)
-    tri_ref[...] = jnp.where(row <= col, aug[:, :n], 0.0) / scale
-    inverse = jnp.where(row >= col, aug[:, n:], 0.0)
-    high = inverse.astype(jnp.bfloat16)
-    low = (inverse - high.astype(jnp.float32)).astype(jnp.bfloat16)
+    lower = lax.broadcasted_iota(jnp.int32, (BLOCK, BLOCK), 0) >= lax.broadcasted_iota(jnp.int32, (BLOCK, BLOCK), 1)
+    upper = lax.broadcasted_iota(jnp.int32, (BLOCK, BLOCK), 0) <= lax.broadcasted_iota(jnp.int32, (BLOCK, BLOCK), 1)
 
     def times(a, b, dims):
         return lax.dot_general(a, b, (dims, ((), ())), preferred_element_type=jnp.float32)
 
-    basis_t = (times(high, panel_ref[...], ((1,), (0,))) + times(low, panel_ref[...], ((1,), (0,)))).astype(jnp.bfloat16)
+    def exact(a, b, contract):
+        return lax.dot_general(a, b, (((contract,), (0,)), ((), ())), precision=EXACT, preferred_element_type=jnp.float32)
+
+    left[...] = gram_ref[...]
+    right[...] = jnp.zeros((n, n), jnp.float32)
+    for o in range(0, n, BLOCK):
+        end = o + BLOCK
+        here = work.at[o // BLOCK]
+        here[:, :BLOCK] = left[o:end, o:end]
+        here[:, BLOCK:] = eye
+        factor_block(here)
+        invert = jnp.where(lower, here[:, BLOCK:], 0.0)
+        right[o:end, o:end] = invert
+        if o:
+            right[o:end, :o] = exact(invert, right[o:end, :o], 1)
+            tri_ref[o:end, :o] = jnp.zeros((BLOCK, o), jnp.float32)
+        tri_ref[o:end, o:end] = jnp.where(upper, here[:, :BLOCK], 0.0) / scale
+        if end < n:
+            left[o:end, end:] = exact(invert, left[o:end, end:], 1)
+            tri_ref[o:end, end:] = left[o:end, end:] / scale
+            for q in range(end, n, BLOCK):
+                u = left[o:end, q:q + BLOCK]
+                left[q:q + BLOCK, q:] = left[q:q + BLOCK, q:] - exact(u, left[o:end, q:], 0)
+                right[q:q + BLOCK, :end] = right[q:q + BLOCK, :end] - exact(u, right[o:end, :end], 0)
+        inverse = right[o:end, :end]
+        high = inverse.astype(jnp.bfloat16)
+        low = (inverse - high.astype(jnp.float32)).astype(jnp.bfloat16)
+        basis[o:end] = (
+            times(high, panel_ref[:end], ((1,), (0,))) + times(low, panel_ref[:end], ((1,), (0,)))
+        ).astype(jnp.bfloat16)
+        for h in range(2):
+            sums = sums_ref[h, :, :end]
+            weights[h, :, o:end] = (times(sums, high, ((1,), (1,))) + times(sums, low, ((1,), (1,)))).astype(jnp.bfloat16)
+
     s_count, orbitals, r_count, _ = out_ref.shape
     per_half = r_count // 2
     for h in range(2):
         source = flag_ref[2 + h]
-        sums = sums_ref[source]
-        weights_t = (times(sums, high, ((1,), (1,))) + times(sums, low, ((1,), (1,)))).astype(jnp.bfloat16)
-        product = times(weights_t, basis_t, ((1,), (0,)))
+        product = times(weights[source], basis[...], ((1,), (0,)))
         outer[h] = tile_ref[source].astype(jnp.float32) - jnp.where(flag_ref[h] > 0, product, 0.0)
     for s in range(s_count):
         parts = [
@@ -119,8 +127,11 @@
         in_specs=[pl.BlockSpec(memory_space=pltpu.SMEM)] + [whole] * 4,
         out_specs=(whole,) * 2,
         scratch_shapes=[
-            pltpu.VMEM((n, 2 * n), jnp.float32),
-            pltpu.VMEM((BLOCK, 2 * BLOCK), jnp.float32),
+            pltpu.VMEM((n, n), jnp.float32),
+            pltpu.VMEM((n, n), jnp.float32),
+            pltpu.VMEM((n // BLOCK, BLOCK, 2 * BLOCK), jnp.float32),
+            pltpu.VMEM((n, rows), jnp.bfloat16),
+            pltpu.VMEM((2, n, n), jnp.bfloat16),
             pltpu.VMEM((2, n, rows), jnp.float32),
         ],
         compiler_params=pltpu.CompilerParams(vmem_limit_bytes=32 << 20),

time: 129 us -> 121 us (0.938)
  Pallas kernels: 122 us -> 115 us
    pallas_call x1, Pallas kernels: 28.9 us -> 21.1 us  [finish(): pl.pallas_call(functools.partial(finish_kernel, scale), out_shape=(jax.Sh...]
where the time goes in v5:
time: 121 us
  Pallas kernels  115 us (95%)
  other arithmetic  2.51 us (2%)
  local copies, waits for them, and re-layouts  1.94 us (2%)
  between operations  1.43 us (1%)
    pallas_call x1, Pallas kernels, exchange(): pl.pallas_call(exchange_kernel, out_shape=(jax.ShapeDtypeStruct((width, r...  93.6 us
    pallas_call x1, Pallas kernels, finish(): pl.pallas_call(functools.partial(finish_kernel, scale), out_shape=(jax.Sh...  21.1 us

profile of v5, /device:TPU:1, one launch (start us, length us, event | category | flops | bytes accessed | tf_op | source)
XLA Modules:
  0.0 120.6 jit_solution(5726481090400878959)
XLA Ops:
  0.6 0.0 copy-start
  1.4 0.1 pad_add_fusion.flag_ref
  1.5 0.0 copy-done
  1.5 0.1 constant_dynamic-slice_fusion
  1.6 0.1 copy.7
  1.7 2.4 %fusion.1 = bf16[128,8,4,128]{0,1,3,2:T(8,128)(2,1)S(1)} fusion(s32[]{:T(128)S(6)} %select_n.31, bf16[4,128,8,128]{3,2,1,0:T(8,128)(2,1)} %param.3), kind=kLoop, calls=%fused_computation.3 | loop fusion | flops 2097152 | bytes 2097156 | tf_op jit(solution)/shard_map/transpose | solution.py:499
  4.1 1.8 %copy.5 = bf16[128,8,4,128]{3,2,1,0:T(4,128)(2,1)S(1)} copy(bf16[128,8,4,128]{0,1,3,2:T(8,128)(2,1)S(1)} %fusion.1) | data formatting | bytes 2097152 | tf_op jit(solution)/shard_map/transpose | solution.py:499
  5.9 93.6 %regroup_exchange.1 = (bf16[512,512]{1,0:T(8,128)(2,1)S(1)}, bf16[2,512,512]{2,1,0:T(8,128)(2,1)S(1)}, f32[8,8,8,512]{3,2,1,0:T(8,128)S(1)}, bf16[16,2,32,512]{3,2,1,0:T(8,128)(2,1)S(1)}) custom-call(s32[1]{0:T(128)} %bitcast.1.owner_ref, bf16[32,4,2,16,128]{4,3,2,1,0:T(8,128)(2,1)S(1)} %bitcast.9, f32[8,128]{1,0:T(8,128)S(1)} %fusion.3.one_ref), custom_call_target="tpu_custom_call" | custom-call | tf_op jit(solution)/shard_map/regroup_exchange/pallas_call | solution.py:462
  99.4 21.1 %factor_apply.1 = (f32[512,512]{1,0:T(8,128)}, bf16[4,128,8,128]{3,2,1,0:T(8,128)(2,1)}) custom-call(s32[4]{0:T(128)S(1)} %pad_add_fusion.flag_ref, f32[512,512]{1,0:T(8,128)S(1)} %bitcast.10, bf16[2,512,512]{2,1,0:T(8,128)(2,1)S(1)} %bitcast.11, bf16[512,512]{1,0:T(8,128)(2,1)S(1)} %get-tuple-element.10.panel_ref, ...), custom_call_target="tpu_custom_call" | custom-call | flops 2147483648 | bytes 6291456 | tf_op jit(solution)/shard_map/factor_apply/pallas_call | solution.py:121
  (3 shorter events, 0.0 us)
Async XLA Ops:
  0.6 0.9 copy-start

commit v6 on v5

--- a/solution.py
+++ b/solution.py
@@ -12,7 +12,6 @@
 STRIP = 8
 EXACT = lax.Precision.HIGHEST
 MESH = pl.DeviceIdType.MESH
-PIECES = 2
 Y = 8
 
 
@@ -148,9 +147,10 @@
     lax.fori_loop(start, stop, lambda k, c: (body(k), c)[1], 0)
 
 
-def exchange_kernel(owner_ref, x_ref, one_ref, panel_ref, gt_ref, gram_ref, sums_ref,
-                    land, order, picks_a, picks_b, gpart, gin, spart, score, shalf, sin,
-                    a_send, a_recv, p_send, p_recv, q_send, q_recv, c_send, c_recv, g1_send, g1_recv, g2_send, g2_recv,
+def exchange_kernel(owner_ref, x_ref, one_ref, one_panel_ref, panel_ref, gt_ref, gram_ref, sums_ref,
+                    land, order, picks, chosen, raw, gpart, gin, spart, score, shalf, sin,
+                    a_send, a_recv, p_send, p_recv, q_send, q_recv, m_send, m_recv, c_send, c_recv,
+                    g1_send, g1_recv, g2_send, g2_recv,
                     g3_send, g3_recv, h2_send, h2_recv, h3_send, h3_recv, g4_send, g4_recv,
                     s1_send, s1_recv, s2_send, s2_recv, s3_send, s3_recv, s4_send, s4_recv):
     pair = lax.axis_index("pair")
@@ -164,9 +164,7 @@
     part = width // Y
     wide = width // BLOCK
     s_count = x_ref.shape[1]
-    s_piece = s_count // PIECES
     over_last = (((1,), (1,)), ((), ()))
-    picks = (picks_a, picks_b)
 
     def on_pair(src, dst, send, recv, k):
         return pltpu.make_async_remote_copy(
@@ -184,97 +182,84 @@
     pl.semaphore_signal(barrier, inc=1, device_id={"col": (1 - half) * Y + y}, device_id_type=MESH)
     pl.semaphore_wait(barrier, n_pair + Y - 1)
 
-    def first(k, peer, slot):
-        ss = pl.ds(k * s_piece, s_piece)
-        return on_pair(x_ref.at[peer, ss, 0], land.at[0, slot, ss], a_send.at[k], a_recv.at[k], peer)
-
-    def second(peer, slot):
-        return on_pair(x_ref.at[peer, :, 1], land.at[1, slot], a_send.at[PIECES], a_recv.at[PIECES], peer)
-
-    def all_first(k):
-        ss = pl.ds(k * s_piece, s_piece)
-        return on_pair(x_ref.at[1:, ss, 0], land.at[0, 1:, ss], a_send.at[k], a_recv.at[k], other_core)
-
-    def all_second():
-        return on_pair(x_ref.at[1:, :, 1], land.at[1, 1:], a_send.at[PIECES], a_recv.at[PIECES], other_core)
-
-    for k in range(PIECES):
-        each(1, n_pair, lambda d: first(k, wrap(pair + d, n_pair), pair).start())
+    def offer(k):
+        return on_col(x_ref.at[:, k // 2, 0, lax.rem(k, 2)], picks.at[y], p_send.at[0], p_recv.at[0], k)
+
+    def all_offers():
+        return on_col(picks.at[1:], picks.at[1:], p_send.at[0], p_recv.at[0], (1 - half) * Y + y)
+
+    @pl.when(half == 0)
+    def _():
+        each(1, Y, lambda d: offer(wrap(y + d, Y)).start())
+
+    def block(h, peer):
+        return on_pair(x_ref.at[peer, :, h], land.at[pair, :, h], a_send.at[h], a_recv.at[h], peer)
+
+    def all_blocks(h):
+        return on_pair(x_ref.at[1:, :, h], land.at[1:, :, h], a_send.at[h], a_recv.at[h], other_core)
+
+    each(1, n_pair, lambda d: block(0, wrap(pair + d, n_pair)).start())
+    land[pair] = x_ref[pair]
+
+    size = 2 * BLOCK
+    row = lax.broadcasted_iota(jnp.int32, (size, size), 0)
+    col = lax.broadcasted_iota(jnp.int32, (size, size), 1)
+    q, r = row & (BLOCK - 1), row // BLOCK
+    order[...] = (col == (q // 4) * 8 + r * 4 + (q & 3)).astype(jnp.float32).astype(jnp.bfloat16)
+    q_row = lax.broadcasted_iota(jnp.int32, (BLOCK, BLOCK), 0)
+
+    def columns_of(moved, ones, u, s):
+        placed = jnp.dot(order[...], moved.reshape(size, BLOCK), preferred_element_type=jnp.float32)
+        out = []
+        for v in range(2):
+            diagonal = jnp.where(q_row == pair * s_count + s, ones[2 * u + v:2 * u + v + 1, :], 0.0)
+            out.append(diagonal - placed[v * BLOCK:(v + 1) * BLOCK])
+        return jnp.concatenate(out, axis=0).astype(jnp.bfloat16)
+
+    def build(h):
+        ones = one_ref[h * wide:(h + 1) * wide, :]
+        for s in range(s_count):
+            for u in range(2):
+                gt_ref[h, u * size:(u + 1) * size, s * BLOCK:(s + 1) * BLOCK] = columns_of(land[:, s, h, u], ones, u, s)
+
+    def across():
+        return on_col(chosen, chosen, q_send.at[0], q_recv.at[0], (1 - half) * Y + y)
+
+    def deal(peer):
+        return on_pair(chosen.at[peer], raw.at[y, pair], m_send.at[0], m_recv.at[0], peer)
+
+    def all_deals():
+        return on_pair(raw.at[y, 1:], raw.at[y, 1:], m_send.at[0], m_recv.at[0], other_core)
+
+    def gather(k):
+        return on_col(raw.at[y], raw.at[y], c_send.at[0], c_recv.at[0], half * Y + k)
+
+    def all_gathers():
+        return on_col(raw.at[1:], raw.at[1:], c_send.at[0], c_recv.at[0], (1 - half) * Y + y)
+
+    @pl.when(half == 0)
+    def _():
+        picks[y] = x_ref[:, y // 2, 0, lax.rem(y, 2)]
+        all_offers().wait_recv()
+        chosen[...] = picks[owner_ref[0]]
+        across().start()
+
+    @pl.when(half == 1)
+    def _():
+        across().wait_recv()
+
+    each(1, n_pair, lambda d: deal(wrap(pair + d, n_pair)).start())
+    raw[y, pair] = chosen[pair]
+    each(1, n_pair, lambda d: block(1, wrap(pair + d, n_pair)).start())
+    all_deals().wait_recv()
+    each(1, Y, lambda d: gather(wrap(y + d, Y)).start())
     for h in range(2):
-        land[h, pair] = x_ref[pair, :, h]
-
-    row = lax.broadcasted_iota(jnp.int32, (width, width), 0)
-    col = lax.broadcasted_iota(jnp.int32, (width, width), 1)
-    q, r = row & (BLOCK - 1), row // BLOCK
-    order[...] = (col == (q // 4) * 16 + r * 4 + (q & 3)).astype(jnp.float32).astype(jnp.bfloat16)
-    q_row = lax.broadcasted_iota(jnp.int32, (BLOCK, BLOCK), 0)
-
-    def build(h, s):
-        moved = land[h, :, s].reshape(width, BLOCK)
-        placed = jnp.dot(order[...], moved, preferred_element_type=jnp.float32)
-        for r in range(wide):
-            diagonal = jnp.where(q_row == pair * s_count + s, one_ref[pl.ds(h * wide + r, 1), :], 0.0)
-            gt_ref[h, r * BLOCK:(r + 1) * BLOCK, s * BLOCK:(s + 1) * BLOCK] = (
-                diagonal - placed[r * BLOCK:(r + 1) * BLOCK]).astype(jnp.bfloat16)
-
-    span = s_piece * BLOCK
-
-    def block(k, piece):
-        return pl.ds(pl.multiple_of(k * part, part), part), pl.ds(piece * span, span)
-
-    def offer(piece, k, slot):
-        rows, lanes = block(k, piece)
-        return on_col(gt_ref.at[0, rows, lanes], picks[piece].at[slot], p_send.at[piece], p_recv.at[piece], k)
-
-    def across(piece):
-        where = panel_ref.at[block(y, piece)]
-        return on_col(where, where, q_send.at[piece], q_recv.at[piece], (1 - half) * Y + y)
-
-    def gather(piece, k, row):
-        where = panel_ref.at[block(row, piece)]
-        return on_col(where, where, c_send.at[piece], c_recv.at[piece], half * Y + k)
-
-    def all_offers(piece):
-        lanes = pl.ds(piece * span, span)
-        return on_col(gt_ref.at[0, :(Y - 1) * part, lanes], picks[piece].at[1:], p_send.at[piece], p_recv.at[piece],
-                      (1 - half) * Y + y)
-
-    def all_gathers(piece):
-        where = panel_ref.at[:(Y - 1) * part, pl.ds(piece * span, span)]
-        return on_col(where, where, c_send.at[piece], c_recv.at[piece], (1 - half) * Y + y)
-
-    for piece in range(PIECES):
-        all_first(piece).wait_recv()
-        for s in range(piece * s_piece, (piece + 1) * s_piece):
-            build(0, s)
-
-        @pl.when(half == 0)
-        def _():
-            each(1, Y, lambda d: offer(piece, wrap(y + d, Y), y).start())
-            rows, lanes = block(y, piece)
-            picks[piece][y] = gt_ref[0, rows, lanes]
-
-    each(1, n_pair, lambda d: second(wrap(pair + d, n_pair), pair).start())
-
-    for piece in range(PIECES):
-        @pl.when(half == 0)
-        def _():
-            all_offers(piece).wait_recv()
-            rows, lanes = block(y, piece)
-            panel_ref[rows, lanes] = picks[piece][owner_ref[0]]
-            across(piece).start()
-
-        @pl.when(half == 1)
-        def _():
-            across(piece).wait_recv()
-
-        each(1, Y, lambda d: gather(piece, wrap(y + d, Y), y).start())
-
-    all_second().wait_recv()
-    for s in range(s_count):
-        build(1, s)
-    for piece in range(PIECES):
-        all_gathers(piece).wait_recv()
+        all_blocks(h).wait_recv()
+        build(h)
+    all_gathers().wait_recv()
+    for k in range(Y):
+        s, u = k // 2, k % 2
+        panel_ref[u * size:(u + 1) * size, s * BLOCK:(s + 1) * BLOCK] = columns_of(raw[k], one_panel_ref[...], u, s)
 
     chunk = sums_ref.shape[2]
     rows_at_once = 2 * BLOCK
@@ -417,16 +402,15 @@
     g4(0, column(1 - core)).wait_recv()
     arrived_s4().wait_recv()
 
-    for piece in range(PIECES):
-        all_first(piece).wait_send()
-        all_gathers(piece).wait_send()
-
-        @pl.when(half == 0)
-        def _():
-            all_offers(piece).wait_send()
-            across(piece).wait_send()
-
-    all_second().wait_send()
+    @pl.when(half == 0)
+    def _():
+        all_offers().wait_send()
+        across().wait_send()
+
+    all_blocks(0).wait_send()
+    all_blocks(1).wait_send()
+    all_deals().wait_send()
+    all_gathers().wait_send()
     s1().wait_send()
     all_g1().wait_send()
     all_s2().wait_send()
@@ -447,16 +431,16 @@
     s4().wait_send()
 
 
-def exchange(owner, blocks, one_t):
-    n_pair, s_count, _, packed, orbitals = blocks.shape
+def exchange(owner, blocks, one_t, one_panel):
+    n_pair, s_count, _, _, packed, orbitals = blocks.shape
     n_chip = n_pair // 2
-    width = n_pair * packed
+    width = 2 * n_pair * packed
     rows = s_count * orbitals
     chunk = 2 * width // n_pair
     vmem = pl.BlockSpec(memory_space=pltpu.VMEM)
     f32, bf16 = jnp.float32, jnp.bfloat16
     sems = []
-    for send, recv in ((PIECES + 1,) * 2, (PIECES,) * 2, (PIECES,) * 2, (PIECES,) * 2, (1, 1), (1, 1), (n_chip, 1),
+    for send, recv in ((2, 2), (1, 1), (1, 1), (1, 1), (1, 1), (1, 1), (1, 1), (n_chip, 1),
                        (n_chip, 1), (1, 1), (2, 2), (1, 1), (1, 1), (1, 1), (1, 1)):
         sems += [pltpu.SemaphoreType.DMA((send,)), pltpu.SemaphoreType.DMA((recv,))]
     return pl.pallas_call(
@@ -467,12 +451,14 @@
             jax.ShapeDtypeStruct((Y, width // Y // 8, 8, width), f32),
             jax.ShapeDtypeStruct((n_chip, 2, chunk, width), bf16),
         ),
-        in_specs=[pl.BlockSpec(memory_space=pltpu.SMEM), vmem, vmem],
+        in_specs=[pl.BlockSpec(memory_space=pltpu.SMEM), vmem, vmem, vmem],
         out_specs=(vmem,) * 4,
         scratch_shapes=[
-            pltpu.VMEM((2, n_pair, s_count, packed, orbitals), bf16),
-            pltpu.VMEM((width, width), bf16),
-            *[pltpu.VMEM((Y, width // Y, rows // PIECES), bf16)] * PIECES,
+            pltpu.VMEM((n_pair, s_count, 2, 2, packed, orbitals), bf16),
+            pltpu.VMEM((2 * BLOCK, 2 * BLOCK), bf16),
+            pltpu.VMEM((Y, n_pair, packed, orbitals), bf16),
+            pltpu.VMEM((n_pair, packed, orbitals), bf16),
+            pltpu.VMEM((Y, n_pair, packed, orbitals), bf16),
             pltpu.VMEM((width // Y, width), f32),
             pltpu.VMEM((n_pair, 8, BLOCK), f32),
             pltpu.VMEM((n_chip, 2, chunk, width), bf16),
@@ -483,7 +469,7 @@
         ],
         compiler_params=pltpu.CompilerParams(collective_id=0, has_side_effects=True, vmem_limit_bytes=32 << 20),
         name="regroup_exchange",
-    )(owner, blocks, one_t)
+    )(owner, blocks, one_t, one_panel)
 
 
 def per_device(two_rdm, one_rdm, panel_block):
@@ -496,10 +482,11 @@
     owner_col = first_orb // r_count
     within = first_orb % r_count
     turned = lax.dynamic_slice_in_dim(jnp.concatenate([two_rdm, two_rdm], 2), within, r_count, 2)
-    blocks = jnp.transpose(turned, (3, 2, 0, 1)).reshape(groups, s_count, 2, RPAN * q_count, orbitals)
+    blocks = jnp.transpose(turned, (3, 2, 0, 1)).reshape(groups, s_count, 2, 2, RPAN * q_count // 2, orbitals)
     one_cols = lax.dynamic_slice_in_dim(one_rdm, col_index * r_count, r_count, 1)
     one_t = lax.dynamic_slice_in_dim(jnp.concatenate([one_cols, one_cols], 1), within, r_count, 1).T
-    panel_t, tile_t, gram, sums_t = exchange(owner_col[None], blocks, one_t)
+    one_panel = lax.dynamic_slice_in_dim(one_rdm, first_orb, RPAN, 1).T
+    panel_t, tile_t, gram, sums_t = exchange(owner_col[None], blocks, one_t, one_panel)
     starts = col_index * r_count + jnp.arange(2, dtype=jnp.int32) * RPAN
     place = (jnp.arange(2, dtype=jnp.int32) + within // RPAN) % 2
     flags = jnp.concatenate([(starts >= first_orb + RPAN).astype(jnp.int32), place])

time: 121 us -> 117 us (0.967)
  Pallas kernels: 115 us -> 111 us
    pallas_call x1, Pallas kernels: 93.6 us -> 89.7 us  [exchange(): pl.pallas_call(exchange_kernel, out_shape=(jax.ShapeDtypeStruct((width, r...]
where the time goes in v6:
time: 117 us
  Pallas kernels  111 us (95%)
  other arithmetic  2.52 us (2%)
  local copies, waits for them, and re-layouts  2.1 us (2%)
  between operations  1.43 us (1%)
    pallas_call x1, Pallas kernels, exchange(): pl.pallas_call(exchange_kernel, out_shape=(jax.ShapeDtypeStruct((width, r...  89.7 us
    pallas_call x1, Pallas kernels, finish(): pl.pallas_call(functools.partial(finish_kernel, scale), out_shape=(jax.Sh...  21.1 us
    transpose x1, other arithmetic, per_device(): jnp.transpose(turned, (3, 2, 0, 1))  2.42 us

profile of v6, /device:TPU:1, one launch (start us, length us, event | category | flops | bytes accessed | tf_op | source)
XLA Modules:
  0.0 116.9 jit_solution(12441833234330990000)
XLA Ops:
  0.6 0.0 copy-start
  1.4 0.1 pad_add_fusion.flag_ref
  1.5 0.0 copy-done
  1.5 0.1 constant_dynamic-slice_fusion.1
  1.6 0.1 copy.8
  1.7 0.1 constant_dynamic-slice_fusion
  1.7 0.1 copy.9
  1.8 2.4 %fusion.1 = bf16[128,8,4,128]{0,1,3,2:T(8,128)(2,1)S(1)} fusion(s32[]{:T(128)S(6)} %select_n.34, bf16[4,128,8,128]{3,2,1,0:T(8,128)(2,1)} %param.3), kind=kLoop, calls=%fused_computation.3 | loop fusion | flops 2097152 | bytes 2097156 | tf_op jit(solution)/shard_map/transpose | solution.py:485
  4.2 1.8 %copy.5 = bf16[128,8,4,128]{3,2,1,0:T(4,128)(2,1)S(1)} copy(bf16[128,8,4,128]{0,1,3,2:T(8,128)(2,1)S(1)} %fusion.1) | data formatting | bytes 2097152 | tf_op jit(solution)/shard_map/transpose | solution.py:485
  6.0 89.7 %regroup_exchange.1 = (bf16[512,512]{1,0:T(8,128)(2,1)S(1)}, bf16[2,512,512]{2,1,0:T(8,128)(2,1)S(1)}, f32[8,8,8,512]{3,2,1,0:T(8,128)S(1)}, bf16[16,2,32,512]{3,2,1,0:T(8,128)(2,1)S(1)}) custom-call(s32[1]{0:T(128)} %bitcast.1.owner_ref, bf16[32,4,2,2,8,128]{5,4,3,2,1,0:T(8,128)(2,1)S(1)} %bitcast.10, f32[8,128]{1,0:T(8,128)S(1)} %fusion.3.one_ref, ...), custom_call_target="tpu_custom_call" | custom-call | tf_op jit(solution)/shard_map/regroup_exchange/pallas_call | solution.py:446
  95.7 21.1 %factor_apply.1 = (f32[512,512]{1,0:T(8,128)}, bf16[4,128,8,128]{3,2,1,0:T(8,128)(2,1)}) custom-call(s32[4]{0:T(128)S(1)} %pad_add_fusion.flag_ref, f32[512,512]{1,0:T(8,128)S(1)} %bitcast.12, bf16[2,512,512]{2,1,0:T(8,128)(2,1)S(1)} %bitcast.13, bf16[512,512]{1,0:T(8,128)(2,1)S(1)} %get-tuple-element.10.panel_ref, ...), custom_call_target="tpu_custom_call" | custom-call | flops 2147483648 | bytes 6291456 | tf_op jit(solution)/shard_map/factor_apply/pallas_call | solution.py:120
  (3 shorter events, 0.0 us)
Async XLA Ops:
  0.6 0.9 copy-start

commit v7 on v6

--- a/solution.py
+++ b/solution.py
@@ -53,25 +53,23 @@
             work[k + STRIP : BLOCK, BLOCK:] = work[k + STRIP : BLOCK, BLOCK:] - delta_b.reshape(below, BLOCK)
 
 
-def finish_kernel(scale, flag_ref, gram_ref, sums_ref, panel_ref, tile_ref, tri_ref, out_ref,
-                  left, right, work, basis, weights, outer):
-    n = gram_ref.shape[0]
+def factor_gram(scale, midway, gram_ref, tri_ref, high_ref, low_ref, left, right, work):
+    n = left.shape[0]
     eye = (
         lax.broadcasted_iota(jnp.int32, (BLOCK, BLOCK), 0) == lax.broadcasted_iota(jnp.int32, (BLOCK, BLOCK), 1)
     ).astype(jnp.float32)
     lower = lax.broadcasted_iota(jnp.int32, (BLOCK, BLOCK), 0) >= lax.broadcasted_iota(jnp.int32, (BLOCK, BLOCK), 1)
     upper = lax.broadcasted_iota(jnp.int32, (BLOCK, BLOCK), 0) <= lax.broadcasted_iota(jnp.int32, (BLOCK, BLOCK), 1)
 
-    def times(a, b, dims):
-        return lax.dot_general(a, b, (dims, ((), ())), preferred_element_type=jnp.float32)
-
     def exact(a, b, contract):
         return lax.dot_general(a, b, (((contract,), (0,)), ((), ())), precision=EXACT, preferred_element_type=jnp.float32)
 
-    left[...] = gram_ref[...]
+    left[...] = gram_ref[...].reshape(n, n)
     right[...] = jnp.zeros((n, n), jnp.float32)
     for o in range(0, n, BLOCK):
         end = o + BLOCK
+        if o == n // 2:
+            midway()
         here = work.at[o // BLOCK]
         here[:, :BLOCK] = left[o:end, o:end]
         here[:, BLOCK:] = eye
@@ -89,21 +87,24 @@
                 u = left[o:end, q:q + BLOCK]
                 left[q:q + BLOCK, q:] = left[q:q + BLOCK, q:] - exact(u, left[o:end, q:], 0)
                 right[q:q + BLOCK, :end] = right[q:q + BLOCK, :end] - exact(u, right[o:end, :end], 0)
-        inverse = right[o:end, :end]
-        high = inverse.astype(jnp.bfloat16)
-        low = (inverse - high.astype(jnp.float32)).astype(jnp.bfloat16)
-        basis[o:end] = (
-            times(high, panel_ref[:end], ((1,), (0,))) + times(low, panel_ref[:end], ((1,), (0,)))
-        ).astype(jnp.bfloat16)
-        for h in range(2):
-            sums = sums_ref[h, :, :end]
-            weights[h, :, o:end] = (times(sums, high, ((1,), (1,))) + times(sums, low, ((1,), (1,)))).astype(jnp.bfloat16)
-
+    high = right[...].astype(jnp.bfloat16)
+    high_ref[...] = high
+    low_ref[...] = (right[...] - high.astype(jnp.float32)).astype(jnp.bfloat16)
+
+
+def finish_kernel(flag_ref, high_ref, low_ref, sums_ref, panel_ref, tile_ref, out_ref, outer):
+    def times(a, b, dims):
+        return lax.dot_general(a, b, (dims, ((), ())), preferred_element_type=jnp.float32)
+
+    high, low = high_ref[...], low_ref[...]
+    basis = (times(high, panel_ref[...], ((1,), (0,))) + times(low, panel_ref[...], ((1,), (0,)))).astype(jnp.bfloat16)
     s_count, orbitals, r_count, _ = out_ref.shape
     per_half = r_count // 2
     for h in range(2):
         source = flag_ref[2 + h]
-        product = times(weights[source], basis[...], ((1,), (0,)))
+        sums = sums_ref[source]
+        weights_t = (times(sums, high, ((1,), (1,))) + times(sums, low, ((1,), (1,)))).astype(jnp.bfloat16)
+        product = times(weights_t, basis, ((1,), (0,)))
         outer[h] = tile_ref[source].astype(jnp.float32) - jnp.where(flag_ref[h] > 0, product, 0.0)
     for s in range(s_count):
         parts = [
@@ -113,30 +114,19 @@
         out_ref[s] = jnp.stack(parts, axis=1).astype(jnp.bfloat16)
 
 
-def finish(flags, gram, sums, panel_t, tile_t, s_count, scale):
-    n = gram.shape[0]
-    rows = panel_t.shape[1]
+def finish(flags, high, low, sums, panel_t, tile_t, s_count):
+    n, rows = panel_t.shape
     whole = pl.BlockSpec(memory_space=pltpu.VMEM)
     return pl.pallas_call(
-        functools.partial(finish_kernel, scale),
-        out_shape=(
-            jax.ShapeDtypeStruct((n, n), jnp.float32),
-            jax.ShapeDtypeStruct((s_count, rows // s_count, 2 * n // BLOCK, BLOCK), jnp.bfloat16),
-        ),
-        in_specs=[pl.BlockSpec(memory_space=pltpu.SMEM)] + [whole] * 4,
-        out_specs=(whole,) * 2,
-        scratch_shapes=[
-            pltpu.VMEM((n, n), jnp.float32),
-            pltpu.VMEM((n, n), jnp.float32),
-            pltpu.VMEM((n // BLOCK, BLOCK, 2 * BLOCK), jnp.float32),
-            pltpu.VMEM((n, rows), jnp.bfloat16),
-            pltpu.VMEM((2, n, n), jnp.bfloat16),
-            pltpu.VMEM((2, n, rows), jnp.float32),
-        ],
-        compiler_params=pltpu.CompilerParams(vmem_limit_bytes=32 << 20),
-        cost_estimate=pl.CostEstimate(flops=16 * n**3, bytes_accessed=24 * n * n, transcendentals=n),
-        name="factor_apply",
-    )(flags, gram, sums, panel_t, tile_t)
+        finish_kernel,
+        out_shape=jax.ShapeDtypeStruct((s_count, rows // s_count, 2 * n // BLOCK, BLOCK), jnp.bfloat16),
+        in_specs=[pl.BlockSpec(memory_space=pltpu.SMEM)] + [whole] * 5,
+        out_specs=whole,
+        scratch_shapes=[pltpu.VMEM((2, n, rows), jnp.float32)],
+        compiler_params=pltpu.CompilerParams(vmem_limit_bytes=24 << 20),
+        cost_estimate=pl.CostEstimate(flops=12 * n**3, bytes_accessed=10 * n * n, transcendentals=0),
+        name="apply",
+    )(flags, high, low, sums, panel_t, tile_t)
 
 
 def wrap(value, count):
@@ -147,8 +137,8 @@
     lax.fori_loop(start, stop, lambda k, c: (body(k), c)[1], 0)
 
 
-def exchange_kernel(owner_ref, x_ref, one_ref, one_panel_ref, panel_ref, gt_ref, gram_ref, sums_ref,
-                    land, order, picks, chosen, raw, gpart, gin, spart, score, shalf, sin,
+def exchange_kernel(scale, owner_ref, x_ref, one_ref, one_panel_ref, panel_ref, gt_ref, sums_ref, tri_ref, high_ref,
+                    low_ref, gram_ref, left, right, work, land, order, picks, chosen, raw, gpart, gin, spart, score, shalf, sin,
                     a_send, a_recv, p_send, p_recv, q_send, q_recv, m_send, m_recv, c_send, c_recv,
                     g1_send, g1_recv, g2_send, g2_recv,
                     g3_send, g3_recv, h2_send, h2_recv, h3_send, h3_recv, g4_send, g4_recv,
@@ -396,10 +386,14 @@
         some_g3(r_tiles).wait_recv()
 
     g4(0, top).start()
-    all_s3().wait_recv()
-    s4().start()
     g4(1, column(3 - core)).wait_recv()
     g4(0, column(1 - core)).wait_recv()
+
+    def midway():
+        all_s3().wait_recv()
+        s4().start()
+
+    factor_gram(scale, midway, gram_ref, tri_ref, high_ref, low_ref, left, right, work)
     arrived_s4().wait_recv()
 
     @pl.when(half == 0)
@@ -431,7 +425,7 @@
     s4().wait_send()
 
 
-def exchange(owner, blocks, one_t, one_panel):
+def exchange(owner, blocks, one_t, one_panel, scale):
     n_pair, s_count, _, _, packed, orbitals = blocks.shape
     n_chip = n_pair // 2
     width = 2 * n_pair * packed
@@ -444,16 +438,22 @@
                        (n_chip, 1), (1, 1), (2, 2), (1, 1), (1, 1), (1, 1), (1, 1)):
         sems += [pltpu.SemaphoreType.DMA((send,)), pltpu.SemaphoreType.DMA((recv,))]
     return pl.pallas_call(
-        exchange_kernel,
+        functools.partial(exchange_kernel, scale),
         out_shape=(
             jax.ShapeDtypeStruct((width, rows), bf16),
             jax.ShapeDtypeStruct((2, width, rows), bf16),
-            jax.ShapeDtypeStruct((Y, width // Y // 8, 8, width), f32),
             jax.ShapeDtypeStruct((n_chip, 2, chunk, width), bf16),
+            jax.ShapeDtypeStruct((width, width), f32),
+            jax.ShapeDtypeStruct((width, width), bf16),
+            jax.ShapeDtypeStruct((width, width), bf16),
         ),
         in_specs=[pl.BlockSpec(memory_space=pltpu.SMEM), vmem, vmem, vmem],
-        out_specs=(vmem,) * 4,
+        out_specs=(vmem,) * 6,
         scratch_shapes=[
+            pltpu.VMEM((Y, width // Y // 8, 8, width), f32),
+            pltpu.VMEM((width, width), f32),
+            pltpu.VMEM((width, width), f32),
+            pltpu.VMEM((width // BLOCK, BLOCK, 2 * BLOCK), f32),
             pltpu.VMEM((n_pair, s_count, 2, 2, packed, orbitals), bf16),
             pltpu.VMEM((2 * BLOCK, 2 * BLOCK), bf16),
             pltpu.VMEM((Y, n_pair, packed, orbitals), bf16),
@@ -486,14 +486,12 @@
     one_cols = lax.dynamic_slice_in_dim(one_rdm, col_index * r_count, r_count, 1)
     one_t = lax.dynamic_slice_in_dim(jnp.concatenate([one_cols, one_cols], 1), within, r_count, 1).T
     one_panel = lax.dynamic_slice_in_dim(one_rdm, first_orb, RPAN, 1).T
-    panel_t, tile_t, gram, sums_t = exchange(owner_col[None], blocks, one_t, one_panel)
+    panel_t, tile_t, sums_t, triangle, high, low = exchange(owner_col[None], blocks, one_t, one_panel, orbitals)
     starts = col_index * r_count + jnp.arange(2, dtype=jnp.int32) * RPAN
     place = (jnp.arange(2, dtype=jnp.int32) + within // RPAN) % 2
     flags = jnp.concatenate([(starts >= first_orb + RPAN).astype(jnp.int32), place])
     sums_t = sums_t.reshape(2, panel_width, panel_width)
-    triangle, updated = finish(
-        flags, gram.reshape(panel_width, panel_width), sums_t, panel_t, tile_t, s_count, orbitals)
-    return updated, triangle
+    return finish(flags, high, low, sums_t, panel_t, tile_t, s_count), triangle
 
 
 def solution(mesh):

time: 117 us -> 113 us (0.966)
  Pallas kernels: 111 us -> 105 us
    pallas_call x2, Pallas kernels: 111 us -> 105 us  [the longest x1 99.8 us: exchange(): pl.pallas_call(functools.partial(exchange_kernel, scale), out_shape=(jax....]
where the time goes in v7:
time: 113 us; the launch traced here: 112 us
  Pallas kernels  105 us (93%)
  local copies, waits for them, and re-layouts  3.06 us (3%)
  other arithmetic  2.52 us (2%)
  between operations  1.43 us (1%)
    pallas_call x1, Pallas kernels, exchange(): pl.pallas_call(functools.partial(exchange_kernel, scale), out_shape=(jax....  99.8 us
    pallas_call x1, Pallas kernels, finish(): pl.pallas_call(finish_kernel, out_shape=jax.ShapeDtypeStruct((s_count, ro...  5.3 us
    transpose x1, other arithmetic, per_device(): jnp.transpose(turned, (3, 2, 0, 1))  2.42 us

profile of v7, /device:TPU:1, one launch (start us, length us, event | category | flops | bytes accessed | tf_op | source)
XLA Modules:
  0.0 112.1 jit_solution(9318578609008125713)
XLA Ops:
  0.6 0.0 copy-start
  1.4 0.1 pad_add_fusion.flag_ref
  1.5 0.0 copy-done
  1.5 0.1 constant_dynamic-slice_fusion.1
  1.6 0.1 copy.8
  1.7 0.1 constant_dynamic-slice_fusion
  1.7 0.1 copy.9
  1.8 2.4 %fusion.1 = bf16[128,8,4,128]{0,1,3,2:T(8,128)(2,1)S(1)} fusion(s32[]{:T(128)S(6)} %select_n.34, bf16[4,128,8,128]{3,2,1,0:T(8,128)(2,1)} %param.3), kind=kLoop, calls=%fused_computation.3 | loop fusion | flops 2097152 | bytes 2097156 | tf_op jit(solution)/shard_map/transpose | solution.py:485
  4.2 1.8 %copy.5 = bf16[128,8,4,128]{3,2,1,0:T(4,128)(2,1)S(1)} copy(bf16[128,8,4,128]{0,1,3,2:T(8,128)(2,1)S(1)} %fusion.1) | data formatting | bytes 2097152 | tf_op jit(solution)/shard_map/transpose | solution.py:485
  6.0 99.8 %regroup_exchange.1 = (bf16[512,512]{1,0:T(8,128)(2,1)S(1)}, bf16[2,512,512]{2,1,0:T(8,128)(2,1)S(1)}, bf16[16,2,32,512]{3,2,1,0:T(8,128)(2,1)S(1)}, f32[512,512...) custom-call(s32[1]{0:T(128)} %bitcast.1.owner_ref, ...), custom_call_target="tpu_custom_call" | custom-call | tf_op jit(solution)/shard_map/regroup_exchange/pallas_call | solution.py:440
  105.9 5.3 %apply.1 = bf16[4,128,8,128]{3,2,1,0:T(8,128)(2,1)} custom-call(s32[4]{0:T(128)S(1)} %pad_add_fusion.flag_ref, bf16[512,512]{1,0:T(8,128)(2,1)S(1)} %get-tuple-element.8.high_ref, bf16[512,512]{1,0:T(8,128)(2,1)S(1)} %get-tuple-element.9.low_ref, bf16[2,512,512]{2,1,0:T(8,128)(2,1)S(1)} %bitcast.11, bf16[512,512]{1,0:T(8,128)(2,1)S(1)} %get-tuple-element.11.panel_ref, ...), custom_call_target="tpu_custom_call" | custom-call | flops 1610612736 | bytes 2621440 | tf_op jit(solution)/shard_map/apply/pallas_call | solution.py:120
  111.2 1.0 copy.12
  (3 shorter events, 0.0 us)
Async XLA Ops:
  0.6 0.9 copy-start
